TPU v7x, 256 devices: a whole 4x4x8 slice. The times are simulated.
256 devices in a mesh: slab: 8 (over x_lo, y), brick: 32 (over x_hi, z, core).
Axes of the slice: x: 4 (x_hi: 2, x_lo: 2; x = x_hi * 2 + x_lo), y: 4, z: 8, core: 2. Of those that a mesh axis runs over, the one named last changes fastest.
Arguments:
- embed: bfloat16 [262144, 512], P(('slab', 'brick')), may hold values from -6 to 6
- cotangent: bfloat16 [262144, 512], P(('slab', 'brick')), may hold values from -6 to 6
- basis: bfloat16 [16, 16, 262144], P(None, None, ('slab', 'brick')), may hold values from -4 to 4
- triplet_row_index: int32 [16, 262144], P(None, ('slab', 'brick')), may hold values from 0 to 1535
- triplet_slot_count: int32 [262144], P(('slab', 'brick')), may hold values from 1 to 16, as said below
- outgoing_edge_rows: int32 [4, 32768], P(None, ('slab', 'brick')), may hold values from 0 to 1023
- residual_weight: bfloat16 [512, 512], replicated, may hold values from -0.25 to 0.25
- down_weight: bfloat16 [512, 64], replicated, may hold values from -0.25 to 0.25
- up_weight: bfloat16 [64, 512], replicated, may hold values from -0.75 to 0.75
- basis_weight: bfloat16 [16, 64], replicated, may hold values from -1.5 to 1.5
Outputs:
- edge_embedding_gradient: bfloat16 [262144, 512], P(('slab', 'brick'))
- residual_weight_gradient: float32 [512, 512], replicated
- down_weight_gradient: float32 [512, 64], replicated
- up_weight_gradient: float32 [64, 512], replicated
- basis_weight_gradient: float32 [16, 64], replicated
Inputs may be any that keep to these rules, and one draw needn't show every extreme that they name: `triplet_row_index`: indices refer to the extended table of the edge's own brick. `triplet_slot_count`: slots at or past the count are empty; in every brick some edge fills all 16 slots; bricks differ in density. `outgoing_edge_rows`: local row numbers within the sending brick; a row may appear more than once.
All inputs are finite; a program needn't handle non-finite values.
Results may differ from a plain program's by a relative error of at most 0.006.
Values may be sent and summed in bfloat16 or wider, within the bound.
A program may use at most 64 MiB of HBM per device.

v0:
```python
import jax
import jax.numpy as jnp
from jax import lax
from jax.sharding import PartitionSpec as P


def passed_along(value, axis, steps):
    count = lax.axis_size(axis)
    pairs = [(source, (source + steps) % count) for source in range(count)]
    return lax.ppermute(value, axis, pairs)


def silu_grad(value):
    sig = jax.nn.sigmoid(value)
    return sig * (1.0 + value * (1.0 - sig))


def selector(index_row, count_rows, dtype):
    positions = lax.broadcasted_iota(jnp.int32, (count_rows, index_row.shape[0]), 0)
    return (positions == index_row[None, :]).astype(dtype)


def shards(
    embed,
    cotangent,
    basis,
    triplet_row_index,
    triplet_slot_count,
    outgoing_edge_rows,
    residual_weight,
    down_weight,
    up_weight,
    basis_weight,
):
    rows = embed.shape[0]
    ghost = outgoing_edge_rows.shape[1]
    trips = triplet_row_index.shape[0]
    res_pre = jnp.dot(embed, residual_weight, preferred_element_type=jnp.float32)
    dres = (cotangent.astype(jnp.float32) * silu_grad(res_pre)).astype(jnp.bfloat16)
    residual_weight_gradient = lax.dot_general(
        embed, dres, (((0,), (0,)), ((), ())), preferred_element_type=jnp.float32
    )
    res_term = lax.dot_general(
        dres, residual_weight, (((1,), (1,)), ((), ())), preferred_element_type=jnp.float32
    )
    pre = lax.dot_general(
        down_weight, embed, (((0,), (1,)), ((), ())), preferred_element_type=jnp.float32
    )
    proj = jax.nn.silu(pre).astype(jnp.bfloat16)
    picks = [selector(outgoing_edge_rows[step], rows, jnp.bfloat16) for step in range(4)]
    received = []
    for step, by in enumerate((1, -1)):
        chosen = jnp.dot(proj, picks[step], preferred_element_type=jnp.float32).astype(jnp.bfloat16)
        received.append(passed_along(chosen, "slab", by))
    for step, by in enumerate((1, -1)):
        chosen = jnp.dot(proj, picks[step + 2], preferred_element_type=jnp.float32).astype(
            jnp.bfloat16
        )
        received.append(passed_along(chosen, "brick", by))
    ghost_proj = jnp.concatenate(received, axis=1)
    edge_table_rows = jnp.concatenate([proj, ghost_proj], axis=1)
    table_rows = edge_table_rows.shape[1]
    weight_list = jnp.einsum("unz,nh->uhz", basis, basis_weight, preferred_element_type=jnp.float32)
    live = (lax.broadcasted_iota(jnp.int32, (trips, rows), 0) < triplet_slot_count[None, :]).astype(
        jnp.float32
    )

    def gather_slot(carry, index_row):
        onehot = selector(index_row, table_rows, jnp.bfloat16)
        picked = jnp.dot(edge_table_rows, onehot, preferred_element_type=jnp.float32).astype(
            jnp.bfloat16
        )
        return (carry, picked)

    _, gathered = lax.scan(gather_slot, jnp.zeros((), jnp.float32), triplet_row_index)
    gathered = gathered.astype(jnp.float32)
    tsum = jnp.sum(weight_list * gathered * live[:, None, :], axis=0)
    activation_value = jax.nn.silu(tsum).astype(jnp.bfloat16)
    dsum = lax.dot_general(
        up_weight, cotangent, (((1,), (1,)), ((), ())), preferred_element_type=jnp.float32
    )
    dt = dsum * silu_grad(tsum)
    up_weight_gradient = lax.dot_general(
        activation_value, cotangent, (((1,), (0,)), ((), ())), preferred_element_type=jnp.float32
    )
    weight_gradient_list = (dt[None, :, :] * gathered * live[:, None, :]).astype(jnp.bfloat16)
    basis_weight_gradient = jnp.einsum(
        "yqi,ywi->qw", basis, weight_gradient_list, preferred_element_type=jnp.float32
    )
    dhx = dt[None, :, :] * weight_list * live[:, None, :]

    def scatter_slot(total, inputs):
        index_row, slot_terms = inputs
        onehot = selector(index_row, table_rows, jnp.float32)
        added = lax.dot_general(
            slot_terms,
            onehot,
            (((1,), (1,)), ((), ())),
            precision=lax.Precision.HIGHEST,
            preferred_element_type=jnp.float32,
        )
        return (total + added, None)

    table_gradient, _ = lax.scan(
        scatter_slot,
        jnp.zeros((edge_table_rows.shape[0], table_rows), jnp.float32),
        (triplet_row_index, dhx),
    )
    dproj = table_gradient[:, :rows]
    for step, by in enumerate((1, -1)):
        block = table_gradient[:, rows + step * ghost : rows + (step + 1) * ghost]
        back = passed_along(block, "slab", -by)
        dproj = dproj + lax.dot_general(
            back,
            picks[step].astype(jnp.float32),
            (((1,), (1,)), ((), ())),
            precision=lax.Precision.HIGHEST,
            preferred_element_type=jnp.float32,
        )
    for step, by in enumerate((1, -1)):
        block = table_gradient[:, rows + (step + 2) * ghost : rows + (step + 3) * ghost]
        back = passed_along(block, "brick", -by)
        dproj = dproj + lax.dot_general(
            back,
            picks[step + 2].astype(jnp.float32),
            (((1,), (1,)), ((), ())),
            precision=lax.Precision.HIGHEST,
            preferred_element_type=jnp.float32,
        )
    dpre = (dproj * silu_grad(pre)).astype(jnp.bfloat16)
    down_weight_gradient = lax.dot_general(
        embed, dpre, (((0,), (1,)), ((), ())), preferred_element_type=jnp.float32
    )
    down_term = lax.dot_general(
        dpre, down_weight, (((0,), (1,)), ((), ())), preferred_element_type=jnp.float32
    )
    edge_embedding_gradient = (res_term + down_term).astype(jnp.bfloat16)
    reduced_total = lax.psum(
        (residual_weight_gradient, down_weight_gradient, up_weight_gradient, basis_weight_gradient),
        ("slab", "brick"),
    )
    return (
        edge_embedding_gradient,
        reduced_total[0],
        reduced_total[1],
        reduced_total[2],
        reduced_total[3],
    )


def solution(mesh):
    in_specs = (
        P(("slab", "brick"), None),
        P(("slab", "brick"), None),
        P(None, None, ("slab", "brick")),
        P(None, ("slab", "brick")),
        P(("slab", "brick")),
        P(None, ("slab", "brick")),
        P(),
        P(),
        P(),
        P(),
    )
    out_specs = (P(("slab", "brick"), None), P(), P(), P(), P())
    return jax.shard_map(shards, mesh=mesh, in_specs=in_specs, out_specs=out_specs, check_vma=False)
```

profile of v0, /device:TPU:1, one launch (start us, length us, event | category | flops | bytes accessed | tf_op | source)
XLA Modules:
  0.0 441.4 jit_solution(11072315548361697162)
XLA Ops:
  16.4 2.7 collective-permute-start.2
  22.8 30.5 %while.21 = (s32[]{:T(128)}, bf16[16,64,1024]{2,1,0:T(8,128)(2,1)S(1)}, s32[16,1024]{1,0:T(8,128)}, bf16[64,1536]{1,0:T(8,128)(2,1)S(1)}, s32[]{:T(128)}) while((s32[]{:T(128)}, bf16[16,64,1024]{2,1,0:T(8,128)(2,1)S(1)}, s32[16,1024]{1,0:T(8,128)}, bf16[64,1536]{1,0:T(8,128)(2,1)S(1)}, s32[]{:T(128)}) %tuple.49), condition=%wide.region_1.2_spmd, body=%wide.region_0.1_spmd.sunk | while | flops 202964992 | bytes 340037 | solution.py:75
  56.1 2.9 fusion.15
  59.0 93.6 %while.22 = (s32[]{:T(128)}, f32[64,1536]{1,0:T(8,128)}, f32[16,64,1024]{2,1,0:T(8,128)}, s32[16,1024]{1,0:T(8,128)}, s32[]{:T(128)}, /*index=5*/s32[]{:T(128)}) while((s32[]{:T(128)}, f32[64,1536]{1,0:T(8,128)}, f32[16,64,1024]{2,1,0:T(8,128)}, s32[16,1024]{1,0:T(8,128)}, s32[]{:T(128)}, /*index=5*/s32[]{:T(128)}) %tuple.59), condition=%wide.region_4.5_spmd.clone, body=%wide.region_3.4_spmd.clone.sunk | while | flops 1209729024 | bytes 1061459 | solution.py:104
  59.8 5.0 %fusion.80 = f32[64,1536]{1,0:T(8,128)} fusion(s32[1024]{0:T(1024)S(1)} %bitcast.73, f32[64,1536]{1,0:T(8,128)} %get-tuple-element.175, f32[16,64,1024]{2,1,0:T(8,128)} %get-tuple-element.182, s32[]{:T(128)} %get-tuple-element.174, pred[]{:T(512)S(6)} %compare.3), kind=kOutput, calls=%fused_computation.10.clone.1 | convolution fusion | flops 1209729024 | bytes 1053185 | tf_op jit(solution)/shard_map/while/body/eval_jaxpr/dot_general | solution.py:95
  65.5 5.1 %fusion.80 = f32[64,1536]{1,0:T(8,128)} fusion(s32[1024]{0:T(1024)S(1)} %bitcast.73, f32[64,1536]{1,0:T(8,128)} %get-tuple-element.175, f32[16,64,1024]{2,1,0:T(8,128)} %get-tuple-element.182, s32[]{:T(128)} %get-tuple-element.174, pred[]{:T(512)S(6)} %compare.3), kind=kOutput, calls=%fused_computation.10.clone.1 | convolution fusion | flops 1209729024 | bytes 1053185 | tf_op jit(solution)/shard_map/while/body/eval_jaxpr/dot_general | solution.py:95
  71.4 5.1 %fusion.80 = f32[64,1536]{1,0:T(8,128)} fusion(s32[1024]{0:T(1024)S(1)} %bitcast.73, f32[64,1536]{1,0:T(8,128)} %get-tuple-element.175, f32[16,64,1024]{2,1,0:T(8,128)} %get-tuple-element.182, s32[]{:T(128)} %get-tuple-element.174, pred[]{:T(512)S(6)} %compare.3), kind=kOutput, calls=%fused_computation.10.clone.1 | convolution fusion | flops 1209729024 | bytes 1053185 | tf_op jit(solution)/shard_map/while/body/eval_jaxpr/dot_general | solution.py:95
  77.3 5.1 %fusion.80 = f32[64,1536]{1,0:T(8,128)} fusion(s32[1024]{0:T(1024)S(1)} %bitcast.73, f32[64,1536]{1,0:T(8,128)} %get-tuple-element.175, f32[16,64,1024]{2,1,0:T(8,128)} %get-tuple-element.182, s32[]{:T(128)} %get-tuple-element.174, pred[]{:T(512)S(6)} %compare.3), kind=kOutput, calls=%fused_computation.10.clone.1 | convolution fusion | flops 1209729024 | bytes 1053185 | tf_op jit(solution)/shard_map/while/body/eval_jaxpr/dot_general | solution.py:95
  83.1 5.1 %fusion.80 = f32[64,1536]{1,0:T(8,128)} fusion(s32[1024]{0:T(1024)S(1)} %bitcast.73, f32[64,1536]{1,0:T(8,128)} %get-tuple-element.175, f32[16,64,1024]{2,1,0:T(8,128)} %get-tuple-element.182, s32[]{:T(128)} %get-tuple-element.174, pred[]{:T(512)S(6)} %compare.3), kind=kOutput, calls=%fused_computation.10.clone.1 | convolution fusion | flops 1209729024 | bytes 1053185 | tf_op jit(solution)/shard_map/while/body/eval_jaxpr/dot_general | solution.py:95
  89.0 5.1 %fusion.80 = f32[64,1536]{1,0:T(8,128)} fusion(s32[1024]{0:T(1024)S(1)} %bitcast.73, f32[64,1536]{1,0:T(8,128)} %get-tuple-element.175, f32[16,64,1024]{2,1,0:T(8,128)} %get-tuple-element.182, s32[]{:T(128)} %get-tuple-element.174, pred[]{:T(512)S(6)} %compare.3), kind=kOutput, calls=%fused_computation.10.clone.1 | convolution fusion | flops 1209729024 | bytes 1053185 | tf_op jit(solution)/shard_map/while/body/eval_jaxpr/dot_general | solution.py:95
  94.8 5.1 %fusion.80 = f32[64,1536]{1,0:T(8,128)} fusion(s32[1024]{0:T(1024)S(1)} %bitcast.73, f32[64,1536]{1,0:T(8,128)} %get-tuple-element.175, f32[16,64,1024]{2,1,0:T(8,128)} %get-tuple-element.182, s32[]{:T(128)} %get-tuple-element.174, pred[]{:T(512)S(6)} %compare.3), kind=kOutput, calls=%fused_computation.10.clone.1 | convolution fusion | flops 1209729024 | bytes 1053185 | tf_op jit(solution)/shard_map/while/body/eval_jaxpr/dot_general | solution.py:95
  100.7 5.1 %fusion.80 = f32[64,1536]{1,0:T(8,128)} fusion(s32[1024]{0:T(1024)S(1)} %bitcast.73, f32[64,1536]{1,0:T(8,128)} %get-tuple-element.175, f32[16,64,1024]{2,1,0:T(8,128)} %get-tuple-element.182, s32[]{:T(128)} %get-tuple-element.174, pred[]{:T(512)S(6)} %compare.3), kind=kOutput, calls=%fused_computation.10.clone.1 | convolution fusion | flops 1209729024 | bytes 1053185 | tf_op jit(solution)/shard_map/while/body/eval_jaxpr/dot_general | solution.py:95
  106.6 5.1 %fusion.80 = f32[64,1536]{1,0:T(8,128)} fusion(s32[1024]{0:T(1024)S(1)} %bitcast.73, f32[64,1536]{1,0:T(8,128)} %get-tuple-element.175, f32[16,64,1024]{2,1,0:T(8,128)} %get-tuple-element.182, s32[]{:T(128)} %get-tuple-element.174, pred[]{:T(512)S(6)} %compare.3), kind=kOutput, calls=%fused_computation.10.clone.1 | convolution fusion | flops 1209729024 | bytes 1053185 | tf_op jit(solution)/shard_map/while/body/eval_jaxpr/dot_general | solution.py:95
  112.4 5.1 %fusion.80 = f32[64,1536]{1,0:T(8,128)} fusion(s32[1024]{0:T(1024)S(1)} %bitcast.73, f32[64,1536]{1,0:T(8,128)} %get-tuple-element.175, f32[16,64,1024]{2,1,0:T(8,128)} %get-tuple-element.182, s32[]{:T(128)} %get-tuple-element.174, pred[]{:T(512)S(6)} %compare.3), kind=kOutput, calls=%fused_computation.10.clone.1 | convolution fusion | flops 1209729024 | bytes 1053185 | tf_op jit(solution)/shard_map/while/body/eval_jaxpr/dot_general | solution.py:95
  118.3 5.1 %fusion.80 = f32[64,1536]{1,0:T(8,128)} fusion(s32[1024]{0:T(1024)S(1)} %bitcast.73, f32[64,1536]{1,0:T(8,128)} %get-tuple-element.175, f32[16,64,1024]{2,1,0:T(8,128)} %get-tuple-element.182, s32[]{:T(128)} %get-tuple-element.174, pred[]{:T(512)S(6)} %compare.3), kind=kOutput, calls=%fused_computation.10.clone.1 | convolution fusion | flops 1209729024 | bytes 1053185 | tf_op jit(solution)/shard_map/while/body/eval_jaxpr/dot_general | solution.py:95
  124.1 5.1 %fusion.80 = f32[64,1536]{1,0:T(8,128)} fusion(s32[1024]{0:T(1024)S(1)} %bitcast.73, f32[64,1536]{1,0:T(8,128)} %get-tuple-element.175, f32[16,64,1024]{2,1,0:T(8,128)} %get-tuple-element.182, s32[]{:T(128)} %get-tuple-element.174, pred[]{:T(512)S(6)} %compare.3), kind=kOutput, calls=%fused_computation.10.clone.1 | convolution fusion | flops 1209729024 | bytes 1053185 | tf_op jit(solution)/shard_map/while/body/eval_jaxpr/dot_general | solution.py:95
  130.0 5.1 %fusion.80 = f32[64,1536]{1,0:T(8,128)} fusion(s32[1024]{0:T(1024)S(1)} %bitcast.73, f32[64,1536]{1,0:T(8,128)} %get-tuple-element.175, f32[16,64,1024]{2,1,0:T(8,128)} %get-tuple-element.182, s32[]{:T(128)} %get-tuple-element.174, pred[]{:T(512)S(6)} %compare.3), kind=kOutput, calls=%fused_computation.10.clone.1 | convolution fusion | flops 1209729024 | bytes 1053185 | tf_op jit(solution)/shard_map/while/body/eval_jaxpr/dot_general | solution.py:95
  135.8 5.1 %fusion.80 = f32[64,1536]{1,0:T(8,128)} fusion(s32[1024]{0:T(1024)S(1)} %bitcast.73, f32[64,1536]{1,0:T(8,128)} %get-tuple-element.175, f32[16,64,1024]{2,1,0:T(8,128)} %get-tuple-element.182, s32[]{:T(128)} %get-tuple-element.174, pred[]{:T(512)S(6)} %compare.3), kind=kOutput, calls=%fused_computation.10.clone.1 | convolution fusion | flops 1209729024 | bytes 1053185 | tf_op jit(solution)/shard_map/while/body/eval_jaxpr/dot_general | solution.py:95
  141.7 5.1 %fusion.80 = f32[64,1536]{1,0:T(8,128)} fusion(s32[1024]{0:T(1024)S(1)} %bitcast.73, f32[64,1536]{1,0:T(8,128)} %get-tuple-element.175, f32[16,64,1024]{2,1,0:T(8,128)} %get-tuple-element.182, s32[]{:T(128)} %get-tuple-element.174, pred[]{:T(512)S(6)} %compare.3), kind=kOutput, calls=%fused_computation.10.clone.1 | convolution fusion | flops 1209729024 | bytes 1053185 | tf_op jit(solution)/shard_map/while/body/eval_jaxpr/dot_general | solution.py:95
  147.6 5.1 %fusion.80 = f32[64,1536]{1,0:T(8,128)} fusion(s32[1024]{0:T(1024)S(1)} %bitcast.73, f32[64,1536]{1,0:T(8,128)} %get-tuple-element.175, f32[16,64,1024]{2,1,0:T(8,128)} %get-tuple-element.182, s32[]{:T(128)} %get-tuple-element.174, pred[]{:T(512)S(6)} %compare.3), kind=kOutput, calls=%fused_computation.10.clone.1 | convolution fusion | flops 1209729024 | bytes 1053185 | tf_op jit(solution)/shard_map/while/body/eval_jaxpr/dot_general | solution.py:95
  153.5 5.6 %collective-permute-start.6 = (f32[64,128]{1,0:T(8,128)S(1)}, f32[64,128]{1,0:T(8,128)S(1)}, u32[]{:S(2)}, u32[]{:S(2)}) collective-permute-start(f32[64,128]{1,0:T(8,128)S(1)} %get-tuple-element.95), channel_id=1, source_target_pairs={{0,31},{1,0},{2,1},{3,2},{4,3},{5,4},{6,5},{7,6},{8,7},{9,8},{10,9... | collective-permute-start | bytes 98312 | tf_op jit(solution)/shard_map/ppermute | solution.py:10
  161.3 3.6 collective-permute-start.4
  170.3 82.2 %psum.31 = f32[16,64]{1,0:T(8,128)} all-reduce(f32[16,64]{1,0:T(8,128)S(1)} %fusion.25), channel_id=1, replica_groups=mesh['slab'=8,'brick'=32] {'slab','brick'}, use_global_device_ids=true, to_apply=%region_8.9 | all-reduce | flops 1024 | bytes 8192 | tf_op jit(solution)/shard_map/psum | solution.py:138
  254.7 176.0 %all-reduce.3.cloned.1.call-done = (f32[512,512]{0,1:T(8,128)}, f32[512,64]{0,1:T(8,128)}, f32[64,512]{1,0:T(8,128)}) async-done(((f32[512,512]{0,1:T(8,128)}, f32[512,64]{0,1:T(8,128)}, f32[64,512]{1,0:T(8,128)}), (f32[512,512]{0,1:T(8,128)}, f32[512,64]{0,1:T(8,128)}, f32[64,512]{1,0:T(8,128)})) %all-reduce.3.cloned.1.call-update) | async-done | bytes 1310736 | tf_op jit(solution)/shard_map/psum | solution.py:138
  (125 shorter events, 72.5 us)
Async XLA Ops:
  7.2 12.4 %copy-start.12 = (bf16[1024,512]{1,0:T(8,128)(2,1)S(1)}, bf16[1024,512]{1,0:T(8,128)(2,1)}, u32[]{:S(2)}) copy-start(bf16[1024,512]{1,0:T(8,128)(2,1)} %param.15) | copy-start | bytes 3145732
  7.2 12.4 %copy-start.3 = (bf16[512,512]{1,0:T(8,128)(2,1)S(1)}, bf16[512,512]{1,0:T(8,128)(2,1)}, u32[]{:S(2)}) copy-start(bf16[512,512]{1,0:T(8,128)(2,1)} %param.20) | copy-start | bytes 1572868
  7.2 423.5 %all-reduce.3.cloned.1.call-start = ((), (), s32[]{:S(2)}) async-start(), calls=%async_computation | async-start | bytes 2621440 | tf_op jit(solution)/shard_map/psum | solution.py:138
  11.3 11.4 %collective-permute-start = (bf16[64,128]{1,0:T(8,128)(2,1)}, bf16[64,128]{1,0:T(8,128)(2,1)S(1)}, u32[]{:S(2)}, u32[]{:S(2)}) collective-permute-start(bf16[64,128]{1,0:T(8,128)(2,1)} %convolution_convert_fusion.3), channel_id=1, source_target_pairs={{0,32},{32,64},{64,96},{96,128},{128,160},{160,192},{192,224},{224... | collective-permute-start | bytes 49160 | tf_op jit(solution)/shard_map/ppermute | solution.py:10
  13.7 9.1 %collective-permute-start.1 = (bf16[64,128]{1,0:T(8,128)(2,1)S(1)}, bf16[64,128]{1,0:T(8,128)(2,1)S(1)}, u32[]{:S(2)}, u32[]{:S(2)}) collective-permute-start(bf16[64,128]{1,0:T(8,128)(2,1)S(1)} %convolution_convert_fusion.2), channel_id=1, source_target_pairs={{0,224},{32,0},{64,32},{96,64},{128,96},{160,128},{192,160},{224,1... | collective-permute-start | bytes 49160 | tf_op jit(solution)/shard_map/ppermute | solution.py:10
  16.4 6.4 %collective-permute-start.2 = (bf16[64,128]{1,0:T(8,128)(2,1)S(1)}, bf16[64,128]{1,0:T(8,128)(2,1)S(1)}, u32[]{:S(2)}, u32[]{:S(2)}) collective-permute-start(bf16[64,128]{1,0:T(8,128)(2,1)S(1)} %convolution_convert_fusion.1), channel_id=1, source_target_pairs={{0,1},{1,2},{2,3},{3,4},{4,5},{5,6},{6,7},{7,8},{8,9},{9,10},{10,1... | collective-permute-start | bytes 49160 | tf_op jit(solution)/shard_map/ppermute | solution.py:10
  19.3 3.4 collective-permute-start.3
  20.9 1.8 copy-start.1
  20.9 1.8 copy-start.11
  22.8 30.5 %copy-start.10 = (bf16[16,64]{1,0:T(8,128)(2,1)S(1)}, bf16[16,64]{1,0:T(8,128)(2,1)}, u32[]{:S(2)}) copy-start(bf16[16,64]{1,0:T(8,128)(2,1)} %param.23) | copy-start | bytes 6148
  53.3 2.3 copy-start.13
  53.3 2.3 copy-start.14
  56.1 2.9 copy-start.5
  152.7 14.3 %copy-start.9 = (f32[64,1536]{1,0:T(8,128)S(1)}, f32[64,1536]{1,0:T(8,128)}, u32[]{:S(2)}) copy-start(f32[64,1536]{1,0:T(8,128)} %get-tuple-element.50) | copy-start | bytes 1179652
  152.7 14.4 %copy-start.15 = (f32[64,1024]{1,0:T(8,128)S(1)}, f32[64,1024]{1,0:T(8,128)}, u32[]{:S(2)}) copy-start(f32[64,1024]{1,0:T(8,128)} %get-tuple-element.100) | copy-start | bytes 786436
  153.5 11.3 %collective-permute-start.6 = (f32[64,128]{1,0:T(8,128)S(1)}, f32[64,128]{1,0:T(8,128)S(1)}, u32[]{:S(2)}, u32[]{:S(2)}) collective-permute-start(f32[64,128]{1,0:T(8,128)S(1)} %get-tuple-element.95), channel_id=1, source_target_pairs={{0,31},{1,0},{2,1},{3,2},{4,3},{5,4},{6,5},{7,6},{8,7},{9,8},{10,9... | collective-permute-start | bytes 98312 | tf_op jit(solution)/shard_map/ppermute | solution.py:10
  161.3 4.9 %collective-permute-start.5 = (f32[64,128]{1,0:T(8,128)S(1)}, f32[64,128]{1,0:T(8,128)S(1)}, u32[]{:S(2)}, u32[]{:S(2)}) collective-permute-start(f32[64,128]{1,0:T(8,128)S(1)} %get-tuple-element.93), channel_id=1, source_target_pairs={{0,32},{32,64},{64,96},{96,128},{128,160},{160,192},{192,224},{224... | collective-permute-start | bytes 98312 | tf_op jit(solution)/shard_map/ppermute | solution.py:10
  161.3 5.3 %collective-permute-start.7 = (f32[64,128]{1,0:T(8,128)S(1)}, f32[64,128]{1,0:T(8,128)S(1)}, u32[]{:S(2)}, u32[]{:S(2)}) collective-permute-start(f32[64,128]{1,0:T(8,128)S(1)} %get-tuple-element.94), channel_id=1, source_target_pairs={{0,1},{1,2},{2,3},{3,4},{4,5},{5,6},{6,7},{7,8},{8,9},{9,10},{10,1... | collective-permute-start | bytes 98312 | tf_op jit(solution)/shard_map/ppermute | solution.py:10
  161.3 5.7 %collective-permute-start.4 = (f32[64,128]{1,0:T(8,128)S(1)}, f32[64,128]{1,0:T(8,128)S(1)}, u32[]{:S(2)}, u32[]{:S(2)}) collective-permute-start(f32[64,128]{1,0:T(8,128)S(1)} %get-tuple-element.92), channel_id=1, source_target_pairs={{0,224},{32,0},{64,32},{96,64},{128,96},{160,128},{192,160},{224,1... | collective-permute-start | bytes 98312 | tf_op jit(solution)/shard_map/ppermute | solution.py:10
  168.5 84.1 %copy-start.8 = (bf16[512,64]{0,1:T(8,128)(2,1)S(1)}, bf16[512,64]{0,1:T(8,128)(2,1)}, u32[]{:S(2)}) copy-start(bf16[512,64]{0,1:T(8,128)(2,1)} %param.21) | copy-start | bytes 196612
  170.3 82.7 %copy-start.2 = (bf16[1024,512]{1,0:T(8,128)(2,1)S(1)}, bf16[1024,512]{1,0:T(8,128)(2,1)}, u32[]{:S(2)}) copy-start(bf16[1024,512]{1,0:T(8,128)(2,1)} %copy-done.1) | copy-start | bytes 3145732
  170.3 82.7 %copy-start.4 = (bf16[512,512]{1,0:T(8,128)(2,1)S(1)}, bf16[512,512]{1,0:T(8,128)(2,1)}, u32[]{:S(2)}) copy-start(bf16[512,512]{1,0:T(8,128)(2,1)} %param.20) | copy-start | bytes 1572868
  430.7 2.6 copy-start.7
  430.7 3.2 copy-start.6
  (1 other events, 1.3 us)
Sparse Core Ops, SparseCore 0:
  168.6 262.0 all-reduce.2
where the time goes:
time: 445 us; the launch traced here: 441 us
  waiting for transfers between devices  177 us (40%)
  matrix products  117 us (26%)
  blocking collectives  82.2 us (18%)
  local copies, waits for them, and re-layouts  30.6 us (7%)
  starting transfers between devices  16.8 us (4%)
  between operations  14.3 us (3%)
    psum x1, waiting for transfers between devices, shards(): lax.psum((residual_weight_gradient, down_weight_gradient, up_weight_gradi...  176 us
    psum x1, blocking collectives, shards(): lax.psum((residual_weight_gradient, down_weight_gradient, up_weight_gradi...  82.2 us
    dot_general x16, matrix products, scatter_slot(): lax.dot_general(slot_terms, onehot, (((1,), (1,)), ((), ())), precision=l...  81.4 us
    dynamic_slice x32, local copies, waits for them, and re-layouts, shards(): lax.scan(gather_slot, jnp.zeros((), jnp.float32), triplet_row_index)  24.5 us
    dot_general x16, matrix products, gather_slot(): jnp.dot(edge_table_rows, onehot, preferred_element_type=jnp.float32)  18 us
    ppermute x8, starting transfers between devices, passed_along(): return lax.ppermute(value, axis, pairs)  16.7 us
  transfers between devices with their start and end apart: 9, of which 2 were waited for; matrix products, arithmetic and copies ran while one was open for 3% of the time, Pallas kernels for 0%

commit v1 on v0

--- a/solution.py
+++ b/solution.py
@@ -1,7 +1,14 @@
+import functools
+
 import jax
 import jax.numpy as jnp
 from jax import lax
+from jax.experimental import pallas as pl
+from jax.experimental.pallas import tpu as pltpu
 from jax.sharding import PartitionSpec as P
+
+MESH = pl.DeviceIdType.MESH
+DMA = pltpu.SemaphoreType.DMA
 
 
 def passed_along(value, axis, steps):
@@ -18,6 +25,223 @@
 def selector(index_row, count_rows, dtype):
     positions = lax.broadcasted_iota(jnp.int32, (count_rows, index_row.shape[0]), 0)
     return (positions == index_row[None, :]).astype(dtype)
+
+
+def where_am_i():
+    slab, brick = lax.axis_index("slab"), lax.axis_index("brick")
+    near = lax.rem(brick, 16)
+    far = slab * 2 + brick // 16
+    return slab, brick, near, far
+
+
+def near_peer(step):
+    slab, brick, near, _ = where_am_i()
+    return slab, (brick // 16) * 16 + lax.rem(near + step, 16)
+
+
+def far_peer(step):
+    _, _, near, far = where_am_i()
+    other = lax.rem(far + step, 16)
+    return other // 2, lax.rem(other, 2) * 16 + near
+
+
+def z_peer(step):
+    slab, brick, near, _ = where_am_i()
+    return slab, (brick // 16) * 16 + lax.rem(near + 2 * step, 16)
+
+
+def core_peer():
+    slab, brick, _, _ = where_am_i()
+    return slab, brick + 1 - 2 * lax.rem(brick, 2)
+
+
+def remote(source, target, send, recv, peer):
+    return pltpu.make_async_remote_copy(
+        src_ref=source, dst_ref=target, send_sem=send, recv_sem=recv,
+        device_id=peer, device_id_type=MESH,
+    )
+
+
+def each(count, body):
+    def step(index, carry):
+        body(index)
+        return carry
+
+    lax.fori_loop(0, count, step, 0)
+
+
+class Exchange:
+    def __init__(self, count, source, target, sems, peer):
+        self.count, self.source, self.target, self.sems, self.peer = count, source, target, sems, peer
+
+    def copy(self, s):
+        send, recv = self.sems
+        return remote(self.source(s), self.target(s), send.at[s], recv.at[s], self.peer(s + 1))
+
+    def start(self):
+        each(self.count, lambda s: self.copy(s).start())
+
+    def arrived(self):
+        each(self.count, lambda s: self.copy(s).wait_recv())
+
+    def sent(self):
+        each(self.count, lambda s: self.copy(s).wait_send())
+
+
+def small_stages(own, got, mid, last, sems):
+    _, _, near, far = where_am_i()
+    scatter = Exchange(
+        15, lambda s: own.at[lax.rem(near + s + 1, 16)], lambda s: got.at[s], sems[0], near_peer
+    )
+    spread = Exchange(15, lambda s: mid.at[far], lambda s: mid.at[far], sems[1], far_peer)
+    gather = Exchange(15, lambda s: last.at[near], lambda s: last.at[near], sems[2], near_peer)
+
+    def middle():
+        scatter.arrived()
+        total = own[near]
+        for s in range(15):
+            total = total + got[s]
+        mid[far] = total
+
+    def final():
+        spread.arrived()
+        total = mid[0]
+        for s in range(1, 16):
+            total = total + mid[s]
+        last[near] = total.astype(last.dtype)
+
+    return scatter, middle, spread, final, gather
+
+
+def announce():
+    slab, brick, _, _ = where_am_i()
+    barrier = pltpu.get_barrier_semaphore()
+
+    def tell(peer):
+        pl.semaphore_signal(barrier, inc=1, device_id=peer, device_id_type=MESH)
+
+    each(15, lambda s: tell(near_peer(s + 1)))
+    each(15, lambda s: tell(far_peer(s + 1)))
+    tell((slab, lax.rem(brick + 1, 32)))
+    tell((slab, lax.rem(brick + 31, 32)))
+    return barrier
+
+
+def reduce_kernel(
+    res_ref, down_ref, up_ref, basis_ref,
+    res_out, down_out, up_out, basis_out,
+    own, got, mid, last, basis_got, basis_mid,
+    half_send, half_got, z_send, z_got, res_mid, res_last, res_other,
+    sem_small, sem_basis, sem_core, sem_z, sem_far,
+):
+    slab, brick, near, far = where_am_i()
+    core, z = lax.rem(near, 2), near // 2
+    barrier = announce()
+    core_rows = pl.multiple_of((1 - core) * 256, 256)
+    half_send[...] = res_ref[pl.ds(core_rows, 256), :].astype(jnp.bfloat16)
+    for s in range(16):
+        own[s, 0:8, :] = down_ref[pl.ds(8 * (s // 2), 8), pl.ds(256 * (s % 2), 256)]
+        own[s, 8:16, :] = up_ref[pl.ds(8 * (s // 2), 8), pl.ds(256 * (s % 2), 256)]
+    pl.semaphore_wait(barrier, 32)
+    core_first = remote(half_send, half_got, sem_core.at[0], sem_core.at[1], core_peer())
+    core_first.start()
+    sems = [(sem_small.at[0, t], sem_small.at[1, t]) for t in range(3)]
+    scatter, middle, spread, final, gather = small_stages(own, got, mid, last, sems)
+    scatter.start()
+    basis_a = Exchange(15, lambda s: basis_ref, lambda s: basis_got.at[near], (sem_basis.at[0, 0], sem_basis.at[1, 0]), near_peer)
+    basis_got[near] = basis_ref[...]
+    basis_a.start()
+    core_first.wait_recv()
+    mine = pl.multiple_of(core * 256, 256)
+    for t in range(8):
+        rows = pl.ds(pl.multiple_of(mine + 32 * t, 32), 32)
+        z_send[t] = (res_ref[rows, :] + half_got[32 * t : 32 * t + 32, :].astype(jnp.float32)).astype(jnp.bfloat16)
+    z_scatter = Exchange(7, lambda s: z_send.at[lax.rem(z + s + 1, 8)], lambda s: z_got.at[s], (sem_z.at[0, 0], sem_z.at[1, 0]), z_peer)
+    z_scatter.start()
+    middle()
+    spread.start()
+    basis_a.arrived()
+    basis_total = basis_got[0]
+    for s in range(1, 16):
+        basis_total = basis_total + basis_got[s]
+    basis_mid[far] = basis_total
+    basis_b = Exchange(15, lambda s: basis_mid.at[far], lambda s: basis_mid.at[far], (sem_basis.at[0, 1], sem_basis.at[1, 1]), far_peer)
+    basis_b.start()
+    z_scatter.arrived()
+    part = res_ref[pl.ds(pl.multiple_of(mine + 32 * z, 32), 32), :] + half_got[pl.ds(pl.multiple_of(32 * z, 32), 32), :].astype(jnp.float32)
+    for s in range(7):
+        part = part + z_got[s].astype(jnp.float32)
+    res_mid[far] = part.astype(jnp.bfloat16)
+    res_spread = Exchange(15, lambda s: res_mid.at[far], lambda s: res_mid.at[far], (sem_far.at[0], sem_far.at[1]), far_peer)
+    res_spread.start()
+    final()
+    gather.start()
+    res_spread.arrived()
+    part = res_mid[0].astype(jnp.float32)
+    for s in range(1, 16):
+        part = part + res_mid[s].astype(jnp.float32)
+    res_last[pl.ds(pl.multiple_of(32 * z, 32), 32), :] = part.astype(jnp.bfloat16)
+    def own_rows(s):
+        return res_last.at[pl.ds(pl.multiple_of(32 * z, 32), 32), :]
+
+    z_gather = Exchange(7, own_rows, own_rows, (sem_z.at[0, 1], sem_z.at[1, 1]), z_peer)
+    z_gather.start()
+    z_gather.arrived()
+    core_last = remote(res_last, res_other, sem_core.at[2], sem_core.at[3], core_peer())
+    core_last.start()
+    res_out[pl.ds(mine, 256), :] = res_last[...].astype(jnp.float32)
+    gather.arrived()
+    for s in range(16):
+        down_out[8 * (s // 2) : 8 * (s // 2) + 8, 256 * (s % 2) : 256 * (s % 2) + 256] = last[s, 0:8, :].astype(jnp.float32)
+        up_out[8 * (s // 2) : 8 * (s // 2) + 8, 256 * (s % 2) : 256 * (s % 2) + 256] = last[s, 8:16, :].astype(jnp.float32)
+    basis_b.arrived()
+    basis_total = basis_mid[0]
+    for s in range(1, 16):
+        basis_total = basis_total + basis_mid[s]
+    basis_out[...] = basis_total
+    core_last.wait_recv()
+    res_out[pl.ds(core_rows, 256), :] = res_other[...].astype(jnp.float32)
+    for exchange in (scatter, spread, gather, basis_a, basis_b, z_scatter, res_spread, z_gather):
+        exchange.sent()
+    core_first.wait_send()
+    core_last.wait_send()
+
+
+def reduce_all(res, down, up, basis):
+    f32, bf16 = jnp.float32, jnp.bfloat16
+    return pl.pallas_call(
+        reduce_kernel,
+        out_shape=(
+            jax.ShapeDtypeStruct((512, 512), f32),
+            jax.ShapeDtypeStruct((64, 512), f32),
+            jax.ShapeDtypeStruct((64, 512), f32),
+            jax.ShapeDtypeStruct((16, 64), f32),
+        ),
+        in_specs=[pl.BlockSpec(memory_space=pltpu.VMEM)] * 4,
+        out_specs=[pl.BlockSpec(memory_space=pltpu.VMEM)] * 4,
+        scratch_shapes=[
+            pltpu.VMEM((16, 16, 256), f32),
+            pltpu.VMEM((15, 16, 256), f32),
+            pltpu.VMEM((16, 16, 256), f32),
+            pltpu.VMEM((16, 16, 256), bf16),
+            pltpu.VMEM((16, 16, 64), f32),
+            pltpu.VMEM((16, 16, 64), f32),
+            pltpu.VMEM((256, 512), bf16),
+            pltpu.VMEM((256, 512), bf16),
+            pltpu.VMEM((8, 32, 512), bf16),
+            pltpu.VMEM((7, 32, 512), bf16),
+            pltpu.VMEM((16, 32, 512), bf16),
+            pltpu.VMEM((256, 512), bf16),
+            pltpu.VMEM((256, 512), bf16),
+            DMA((2, 3, 15)),
+            DMA((2, 2, 15)),
+            DMA((4,)),
+            DMA((2, 2, 7)),
+            DMA((2, 15)),
+        ],
+        compiler_params=pltpu.CompilerParams(collective_id=0, has_side_effects=True),
+        name="reduce_all",
+    )(res, down, up, basis)
 
 
 def shards(
@@ -91,12 +315,11 @@
 
     def scatter_slot(total, inputs):
         index_row, slot_terms = inputs
-        onehot = selector(index_row, table_rows, jnp.float32)
+        onehot = selector(index_row, table_rows, jnp.bfloat16)
         added = lax.dot_general(
-            slot_terms,
+            slot_terms.astype(jnp.bfloat16),
             onehot,
             (((1,), (1,)), ((), ())),
-            precision=lax.Precision.HIGHEST,
             preferred_element_type=jnp.float32,
         )
         return (total + added, None)
@@ -129,20 +352,19 @@
         )
     dpre = (dproj * silu_grad(pre)).astype(jnp.bfloat16)
     down_weight_gradient = lax.dot_general(
-        embed, dpre, (((0,), (1,)), ((), ())), preferred_element_type=jnp.float32
+        dpre, embed, (((1,), (0,)), ((), ())), preferred_element_type=jnp.float32
     )
     down_term = lax.dot_general(
         dpre, down_weight, (((0,), (1,)), ((), ())), preferred_element_type=jnp.float32
     )
     edge_embedding_gradient = (res_term + down_term).astype(jnp.bfloat16)
-    reduced_total = lax.psum(
-        (residual_weight_gradient, down_weight_gradient, up_weight_gradient, basis_weight_gradient),
-        ("slab", "brick"),
+    reduced_total = reduce_all(
+        residual_weight_gradient, down_weight_gradient, up_weight_gradient, basis_weight_gradient
     )
     return (
         edge_embedding_gradient,
         reduced_total[0],
-        reduced_total[1],
+        reduced_total[1].T,
         reduced_total[2],
         reduced_total[3],
     )

time: 445 us -> 185 us (0.42)
  waiting for transfers between devices: 177 us -> 0.89 us
  blocking collectives: 82.2 us -> 0 us
  Pallas kernels: 0 us -> 47 us
  matrix products: 117 us -> 85.6 us
  between operations: 14.3 us -> 0.93 us
    psum x1 -> x0, waiting for transfers between devices: 176 us -> none  [shards(): lax.psum((residual_weight_gradient, down_weight_gradient, up_weight_gradi...]
    psum x1 -> x0, blocking collectives: 82.2 us -> none  [shards(): lax.psum((residual_weight_gradient, down_weight_gradient, up_weight_gradi...]
    pallas_call x0 -> x1, Pallas kernels: none -> 47 us  [reduce_all(): pl.pallas_call(reduce_kernel, out_shape=(jax.ShapeDtypeStruct((512, 512),...]
    dot_general x17, matrix products: 82.3 us -> 49.6 us  [the longest x16 48.6 us: scatter_slot(): lax.dot_general(slot_terms.astype(jnp.bfloat16), onehot, (((1,), (1,)), (...]
  transfers between devices with their start and end apart: 9 -> 8, of which waited for: 2 -> 1; matrix products, arithmetic and copies ran while one was open for 3% -> 4% of each run, Pallas kernels for 0% -> 0%
where the time goes in v1:
time: 185 us; the launch traced here: 182 us
  matrix products  85.6 us (46%)
  Pallas kernels  47 us (25%)
  local copies, waits for them, and re-layouts  29.7 us (16%)
  starting transfers between devices  16.7 us (9%)
    dot_general x16, matrix products, scatter_slot(): lax.dot_general(slot_terms.astype(jnp.bfloat16), onehot, (((1,), (1,)), (...  48.6 us
    pallas_call x1, Pallas kernels, reduce_all(): pl.pallas_call(reduce_kernel, out_shape=(jax.ShapeDtypeStruct((512, 512),...  47 us
    dynamic_slice x32, local copies, waits for them, and re-layouts, shards(): lax.scan(gather_slot, jnp.zeros((), jnp.float32), triplet_row_index)  24.5 us
    dot_general x16, matrix products, gather_slot(): jnp.dot(edge_table_rows, onehot, preferred_element_type=jnp.float32)  18 us
    ppermute x8, starting transfers between devices, passed_along(): return lax.ppermute(value, axis, pairs)  16.7 us
  transfers between devices with their start and end apart: 8, of which 1 were waited for; matrix products, arithmetic and copies ran while one was open for 4% of the time, Pallas kernels for 0%

profile of v1, /device:TPU:1, one launch (start us, length us, event | category | flops | bytes accessed | tf_op | source)
XLA Modules:
  0.0 181.8 jit_solution(12329667711958773905)
XLA Ops:
  7.1 2.4 %collective-permute-start.1 = (bf16[64,128]{1,0:T(8,128)(2,1)S(1)}, bf16[64,128]{1,0:T(8,128)(2,1)S(1)}, u32[]{:S(2)}, u32[]{:S(2)}) collective-permute-start(bf16[64,128]{1,0:T(8,128)(2,1)S(1)} %convolution_convert_fusion.2), channel_id=1, source_target_pairs={{0,224},{32,0},{64,32},{96,64},{128,96},{160,128},{192,160},{224,1... | collective-permute-start | bytes 49160 | tf_op jit(solution)/shard_map/ppermute | solution.py:17
  9.8 2.7 %collective-permute-start.2 = (bf16[64,128]{1,0:T(8,128)(2,1)S(1)}, bf16[64,128]{1,0:T(8,128)(2,1)S(1)}, u32[]{:S(2)}, u32[]{:S(2)}) collective-permute-start(bf16[64,128]{1,0:T(8,128)(2,1)S(1)} %convolution_convert_fusion.1), channel_id=1, source_target_pairs={{0,1},{1,2},{2,3},{3,4},{4,5},{5,6},{6,7},{7,8},{8,9},{9,10},{10,1... | collective-permute-start | bytes 49160 | tf_op jit(solution)/shard_map/ppermute | solution.py:17
  16.3 30.5 %while.21 = (s32[]{:T(128)}, bf16[16,64,1024]{2,1,0:T(8,128)(2,1)S(1)}, s32[16,1024]{1,0:T(8,128)}, bf16[64,1536]{1,0:T(8,128)(2,1)S(1)}, s32[]{:T(128)}) while((s32[]{:T(128)}, bf16[16,64,1024]{2,1,0:T(8,128)(2,1)S(1)}, s32[16,1024]{1,0:T(8,128)}, bf16[64,1536]{1,0:T(8,128)(2,1)S(1)}, s32[]{:T(128)}) %tuple.48), condition=%wide.region_1.2_spmd, body=%wide.region_0.1_spmd.sunk | while | flops 202964992 | bytes 340037 | solution.py:299
  46.8 2.3 %fusion.12 = (f32[64,1024]{1,0:T(8,128)S(1)}, f32[64,16,1024]{2,0,1:T(8,128)S(1)}) fusion(bf16[16,64,1024]{2,1,0:T(8,128)(2,1)S(1)} %get-tuple-element.53, f32[16,1024]{1,0:T(8,128)S(1)} %fusion.41, bf16[16,16,1024]{2,1,0:T(8,128)(2,1)} %param.16, bf16[16,64]{1,0:T(8,128)(2,1)S(1)} %copy-done.10), kind=kOutput, calls=%fused_computation.18 | convolution fusion | flops 37683200 | bytes 7145472 | tf_op jit(solution)/shard_map/unz,nh->uhz/dot_general | solution.py:287
  51.5 60.9 %while.22 = (s32[]{:T(128)}, f32[64,1536]{1,0:T(8,128)}, bf16[16,64,1024]{2,1,0:T(8,128)(2,1)S(1)}, s32[16,1024]{1,0:T(8,128)}, s32[]{:T(128)}, /*index=5*/s32[]{:T(128)}) while((s32[]{:T(128)}, f32[64,1536]{1,0:T(8,128)}, bf16[16,64,1024]{2,1,0:T(8,128)(2,1)S(1)}, s32[16,1024]{1,0:T(8,128)}, s32[]{:T(128)}, ...), condition=%wide.region_4.5_spmd.clone, body=%wide.region_3.4_spmd.clone.sunk | while | flops 203096064 | bytes 929879 | solution.py:327
  55.2 3.1 %fusion.81 = f32[64,1536]{1,0:T(8,128)} fusion(s32[1024]{0:T(1024)S(1)} %bitcast.73, f32[64,1536]{1,0:T(8,128)} %get-tuple-element.175, pred[]{:T(512)S(6)} %compare.3, bf16[16,64,1024]{2,1,0:T(8,128)(2,1)S(1)} %get-tuple-element.182, s32[]{:T(128)} %get-tuple-element.174), kind=kOutput, calls=%fused_computation.10.clone.1 | convolution fusion | flops 203096064 | bytes 921605 | tf_op jit(solution)/shard_map/while/body/eval_jaxpr/dot_general | solution.py:319
  59.1 3.1 %fusion.81 = f32[64,1536]{1,0:T(8,128)} fusion(s32[1024]{0:T(1024)S(1)} %bitcast.73, f32[64,1536]{1,0:T(8,128)} %get-tuple-element.175, pred[]{:T(512)S(6)} %compare.3, bf16[16,64,1024]{2,1,0:T(8,128)(2,1)S(1)} %get-tuple-element.182, s32[]{:T(128)} %get-tuple-element.174), kind=kOutput, calls=%fused_computation.10.clone.1 | convolution fusion | flops 203096064 | bytes 921605 | tf_op jit(solution)/shard_map/while/body/eval_jaxpr/dot_general | solution.py:319
  62.9 3.1 %fusion.81 = f32[64,1536]{1,0:T(8,128)} fusion(s32[1024]{0:T(1024)S(1)} %bitcast.73, f32[64,1536]{1,0:T(8,128)} %get-tuple-element.175, pred[]{:T(512)S(6)} %compare.3, bf16[16,64,1024]{2,1,0:T(8,128)(2,1)S(1)} %get-tuple-element.182, s32[]{:T(128)} %get-tuple-element.174), kind=kOutput, calls=%fused_computation.10.clone.1 | convolution fusion | flops 203096064 | bytes 921605 | tf_op jit(solution)/shard_map/while/body/eval_jaxpr/dot_general | solution.py:319
  66.8 3.1 %fusion.81 = f32[64,1536]{1,0:T(8,128)} fusion(s32[1024]{0:T(1024)S(1)} %bitcast.73, f32[64,1536]{1,0:T(8,128)} %get-tuple-element.175, pred[]{:T(512)S(6)} %compare.3, bf16[16,64,1024]{2,1,0:T(8,128)(2,1)S(1)} %get-tuple-element.182, s32[]{:T(128)} %get-tuple-element.174), kind=kOutput, calls=%fused_computation.10.clone.1 | convolution fusion | flops 203096064 | bytes 921605 | tf_op jit(solution)/shard_map/while/body/eval_jaxpr/dot_general | solution.py:319
  70.7 3.1 %fusion.81 = f32[64,1536]{1,0:T(8,128)} fusion(s32[1024]{0:T(1024)S(1)} %bitcast.73, f32[64,1536]{1,0:T(8,128)} %get-tuple-element.175, pred[]{:T(512)S(6)} %compare.3, bf16[16,64,1024]{2,1,0:T(8,128)(2,1)S(1)} %get-tuple-element.182, s32[]{:T(128)} %get-tuple-element.174), kind=kOutput, calls=%fused_computation.10.clone.1 | convolution fusion | flops 203096064 | bytes 921605 | tf_op jit(solution)/shard_map/while/body/eval_jaxpr/dot_general | solution.py:319
  74.5 3.1 %fusion.81 = f32[64,1536]{1,0:T(8,128)} fusion(s32[1024]{0:T(1024)S(1)} %bitcast.73, f32[64,1536]{1,0:T(8,128)} %get-tuple-element.175, pred[]{:T(512)S(6)} %compare.3, bf16[16,64,1024]{2,1,0:T(8,128)(2,1)S(1)} %get-tuple-element.182, s32[]{:T(128)} %get-tuple-element.174), kind=kOutput, calls=%fused_computation.10.clone.1 | convolution fusion | flops 203096064 | bytes 921605 | tf_op jit(solution)/shard_map/while/body/eval_jaxpr/dot_general | solution.py:319
  78.4 3.1 %fusion.81 = f32[64,1536]{1,0:T(8,128)} fusion(s32[1024]{0:T(1024)S(1)} %bitcast.73, f32[64,1536]{1,0:T(8,128)} %get-tuple-element.175, pred[]{:T(512)S(6)} %compare.3, bf16[16,64,1024]{2,1,0:T(8,128)(2,1)S(1)} %get-tuple-element.182, s32[]{:T(128)} %get-tuple-element.174), kind=kOutput, calls=%fused_computation.10.clone.1 | convolution fusion | flops 203096064 | bytes 921605 | tf_op jit(solution)/shard_map/while/body/eval_jaxpr/dot_general | solution.py:319
  82.3 3.1 %fusion.81 = f32[64,1536]{1,0:T(8,128)} fusion(s32[1024]{0:T(1024)S(1)} %bitcast.73, f32[64,1536]{1,0:T(8,128)} %get-tuple-element.175, pred[]{:T(512)S(6)} %compare.3, bf16[16,64,1024]{2,1,0:T(8,128)(2,1)S(1)} %get-tuple-element.182, s32[]{:T(128)} %get-tuple-element.174), kind=kOutput, calls=%fused_computation.10.clone.1 | convolution fusion | flops 203096064 | bytes 921605 | tf_op jit(solution)/shard_map/while/body/eval_jaxpr/dot_general | solution.py:319
  86.1 3.1 %fusion.81 = f32[64,1536]{1,0:T(8,128)} fusion(s32[1024]{0:T(1024)S(1)} %bitcast.73, f32[64,1536]{1,0:T(8,128)} %get-tuple-element.175, pred[]{:T(512)S(6)} %compare.3, bf16[16,64,1024]{2,1,0:T(8,128)(2,1)S(1)} %get-tuple-element.182, s32[]{:T(128)} %get-tuple-element.174), kind=kOutput, calls=%fused_computation.10.clone.1 | convolution fusion | flops 203096064 | bytes 921605 | tf_op jit(solution)/shard_map/while/body/eval_jaxpr/dot_general | solution.py:319
  90.0 3.1 %fusion.81 = f32[64,1536]{1,0:T(8,128)} fusion(s32[1024]{0:T(1024)S(1)} %bitcast.73, f32[64,1536]{1,0:T(8,128)} %get-tuple-element.175, pred[]{:T(512)S(6)} %compare.3, bf16[16,64,1024]{2,1,0:T(8,128)(2,1)S(1)} %get-tuple-element.182, s32[]{:T(128)} %get-tuple-element.174), kind=kOutput, calls=%fused_computation.10.clone.1 | convolution fusion | flops 203096064 | bytes 921605 | tf_op jit(solution)/shard_map/while/body/eval_jaxpr/dot_general | solution.py:319
  93.8 3.1 %fusion.81 = f32[64,1536]{1,0:T(8,128)} fusion(s32[1024]{0:T(1024)S(1)} %bitcast.73, f32[64,1536]{1,0:T(8,128)} %get-tuple-element.175, pred[]{:T(512)S(6)} %compare.3, bf16[16,64,1024]{2,1,0:T(8,128)(2,1)S(1)} %get-tuple-element.182, s32[]{:T(128)} %get-tuple-element.174), kind=kOutput, calls=%fused_computation.10.clone.1 | convolution fusion | flops 203096064 | bytes 921605 | tf_op jit(solution)/shard_map/while/body/eval_jaxpr/dot_general | solution.py:319
  97.7 3.1 %fusion.81 = f32[64,1536]{1,0:T(8,128)} fusion(s32[1024]{0:T(1024)S(1)} %bitcast.73, f32[64,1536]{1,0:T(8,128)} %get-tuple-element.175, pred[]{:T(512)S(6)} %compare.3, bf16[16,64,1024]{2,1,0:T(8,128)(2,1)S(1)} %get-tuple-element.182, s32[]{:T(128)} %get-tuple-element.174), kind=kOutput, calls=%fused_computation.10.clone.1 | convolution fusion | flops 203096064 | bytes 921605 | tf_op jit(solution)/shard_map/while/body/eval_jaxpr/dot_general | solution.py:319
  101.6 3.1 %fusion.81 = f32[64,1536]{1,0:T(8,128)} fusion(s32[1024]{0:T(1024)S(1)} %bitcast.73, f32[64,1536]{1,0:T(8,128)} %get-tuple-element.175, pred[]{:T(512)S(6)} %compare.3, bf16[16,64,1024]{2,1,0:T(8,128)(2,1)S(1)} %get-tuple-element.182, s32[]{:T(128)} %get-tuple-element.174), kind=kOutput, calls=%fused_computation.10.clone.1 | convolution fusion | flops 203096064 | bytes 921605 | tf_op jit(solution)/shard_map/while/body/eval_jaxpr/dot_general | solution.py:319
  105.4 3.1 %fusion.81 = f32[64,1536]{1,0:T(8,128)} fusion(s32[1024]{0:T(1024)S(1)} %bitcast.73, f32[64,1536]{1,0:T(8,128)} %get-tuple-element.175, pred[]{:T(512)S(6)} %compare.3, bf16[16,64,1024]{2,1,0:T(8,128)(2,1)S(1)} %get-tuple-element.182, s32[]{:T(128)} %get-tuple-element.174), kind=kOutput, calls=%fused_computation.10.clone.1 | convolution fusion | flops 203096064 | bytes 921605 | tf_op jit(solution)/shard_map/while/body/eval_jaxpr/dot_general | solution.py:319
  109.3 3.1 %fusion.81 = f32[64,1536]{1,0:T(8,128)} fusion(s32[1024]{0:T(1024)S(1)} %bitcast.73, f32[64,1536]{1,0:T(8,128)} %get-tuple-element.175, pred[]{:T(512)S(6)} %compare.3, bf16[16,64,1024]{2,1,0:T(8,128)(2,1)S(1)} %get-tuple-element.182, s32[]{:T(128)} %get-tuple-element.174), kind=kOutput, calls=%fused_computation.10.clone.1 | convolution fusion | flops 203096064 | bytes 921605 | tf_op jit(solution)/shard_map/while/body/eval_jaxpr/dot_general | solution.py:319
  113.3 5.6 %collective-permute-start.6 = (f32[64,128]{1,0:T(8,128)S(1)}, f32[64,128]{1,0:T(8,128)S(1)}, u32[]{:S(2)}, u32[]{:S(2)}) collective-permute-start(f32[64,128]{1,0:T(8,128)S(1)} %get-tuple-element.95), channel_id=1, source_target_pairs={{0,31},{1,0},{2,1},{3,2},{4,3},{5,4},{6,5},{7,6},{8,7},{9,8},{10,9... | collective-permute-start | bytes 98312 | tf_op jit(solution)/shard_map/ppermute | solution.py:17
  121.1 3.6 %collective-permute-start.4 = (f32[64,128]{1,0:T(8,128)S(1)}, f32[64,128]{1,0:T(8,128)S(1)}, u32[]{:S(2)}, u32[]{:S(2)}) collective-permute-start(f32[64,128]{1,0:T(8,128)S(1)} %get-tuple-element.92), channel_id=1, source_target_pairs={{0,224},{32,0},{64,32},{96,64},{128,96},{160,128},{192,160},{224,1... | collective-permute-start | bytes 98312 | tf_op jit(solution)/shard_map/ppermute | solution.py:17
  128.7 47.0 %reduce_all.1 = (f32[512,512]{1,0:T(8,128)}, f32[64,512]{1,0:T(8,128)}, f32[64,512]{1,0:T(8,128)}, f32[16,64]{1,0:T(8,128)}) custom-call(f32[512,512]{1,0:T(8,128)} %convolution_bitcast_fusion.res_ref, f32[64,512]{1,0:T(8,128)} %fusion.47.down_ref, f32[64,512]{1,0:T(8,128)} %fusion.39.up_ref, f32[16,64]{1,0:T(8,128)} %fusion.25.basis_ref), custom_call_target="tpu_custom_call" | custom-call | tf_op jit(solution)/shard_map/reduce_all/pallas_call | solution.py:212
  175.7 3.2 %add_convert_fusion = bf16[1024,512]{1,0:T(8,128)(2,1)} fusion(f32[1024,512]{1,0:T(8,128)S(1)} %fusion.46, bf16[1024,512]{1,0:T(8,128)(2,1)} %copy-done.2, bf16[512,512]{1,0:T(8,128)(2,1)} %param.20), kind=kOutput, calls=%fused_computation.24 | convolution fusion | flops 537919488 | bytes 4718592 | tf_op jit(solution)/shard_map/dot_general | solution.py:267
  (123 shorter events, 67.3 us)
Async XLA Ops:
  0.6 1.3 copy-start
  0.6 12.4 %copy-start.12 = (bf16[1024,512]{1,0:T(8,128)(2,1)S(1)}, bf16[1024,512]{1,0:T(8,128)(2,1)}, u32[]{:S(2)}) copy-start(bf16[1024,512]{1,0:T(8,128)(2,1)} %param.15) | copy-start | bytes 3145732
  0.7 12.4 %copy-start.4 = (bf16[512,512]{1,0:T(8,128)(2,1)S(1)}, bf16[512,512]{1,0:T(8,128)(2,1)}, u32[]{:S(2)}) copy-start(bf16[512,512]{1,0:T(8,128)(2,1)} %param.20) | copy-start | bytes 1572868
  4.8 11.4 %collective-permute-start = (bf16[64,128]{1,0:T(8,128)(2,1)}, bf16[64,128]{1,0:T(8,128)(2,1)S(1)}, u32[]{:S(2)}, u32[]{:S(2)}) collective-permute-start(bf16[64,128]{1,0:T(8,128)(2,1)} %convolution_convert_fusion.3), channel_id=1, source_target_pairs={{0,32},{32,64},{64,96},{96,128},{128,160},{160,192},{192,224},{224... | collective-permute-start | bytes 49160 | tf_op jit(solution)/shard_map/ppermute | solution.py:17
  7.1 9.1 %collective-permute-start.1 = (bf16[64,128]{1,0:T(8,128)(2,1)S(1)}, bf16[64,128]{1,0:T(8,128)(2,1)S(1)}, u32[]{:S(2)}, u32[]{:S(2)}) collective-permute-start(bf16[64,128]{1,0:T(8,128)(2,1)S(1)} %convolution_convert_fusion.2), channel_id=1, source_target_pairs={{0,224},{32,0},{64,32},{96,64},{128,96},{160,128},{192,160},{224,1... | collective-permute-start | bytes 49160 | tf_op jit(solution)/shard_map/ppermute | solution.py:17
  9.8 6.4 %collective-permute-start.2 = (bf16[64,128]{1,0:T(8,128)(2,1)S(1)}, bf16[64,128]{1,0:T(8,128)(2,1)S(1)}, u32[]{:S(2)}, u32[]{:S(2)}) collective-permute-start(bf16[64,128]{1,0:T(8,128)(2,1)S(1)} %convolution_convert_fusion.1), channel_id=1, source_target_pairs={{0,1},{1,2},{2,3},{3,4},{4,5},{5,6},{6,7},{7,8},{8,9},{9,10},{10,1... | collective-permute-start | bytes 49160 | tf_op jit(solution)/shard_map/ppermute | solution.py:17
  12.8 3.4 %collective-permute-start.3 = (bf16[64,128]{1,0:T(8,128)(2,1)S(1)}, bf16[64,128]{1,0:T(8,128)(2,1)S(1)}, u32[]{:S(2)}, u32[]{:S(2)}) collective-permute-start(bf16[64,128]{1,0:T(8,128)(2,1)S(1)} %convolution_convert_fusion), channel_id=1, source_target_pairs={{0,31},{1,0},{2,1},{3,2},{4,3},{5,4},{6,5},{7,6},{8,7},{9,8},{10,9... | collective-permute-start | bytes 49160 | tf_op jit(solution)/shard_map/ppermute | solution.py:17
  14.3 1.8 copy-start.2
  14.4 1.7 copy-start.11
  16.2 30.5 %copy-start.10 = (bf16[16,64]{1,0:T(8,128)(2,1)S(1)}, bf16[16,64]{1,0:T(8,128)(2,1)}, u32[]{:S(2)}) copy-start(bf16[16,64]{1,0:T(8,128)(2,1)} %param.23) | copy-start | bytes 6148
  46.7 2.4 %copy-start.13 = (bf16[1024,512]{1,0:T(8,128)(2,1)S(1)}, bf16[1024,512]{1,0:T(8,128)(2,1)}, u32[]{:S(2)}) copy-start(bf16[1024,512]{1,0:T(8,128)(2,1)} %param.15) | copy-start | bytes 3145732
  46.8 2.4 %copy-start.14 = (bf16[64,512]{1,0:T(8,128)(2,1)S(1)}, bf16[64,512]{1,0:T(8,128)(2,1)}, u32[]{:S(2)}) copy-start(bf16[64,512]{1,0:T(8,128)(2,1)} %param.22) | copy-start | bytes 196612
  46.8 2.8 %copy-start.3 = (bf16[16,16,1024]{2,1,0:T(8,128)(2,1)S(1)}, bf16[16,16,1024]{2,1,0:T(8,128)(2,1)}, u32[]{:S(2)}) copy-start(bf16[16,16,1024]{2,1,0:T(8,128)(2,1)} %param.16) | copy-start | bytes 1572868
  112.4 14.4 %copy-start.8 = (f32[64,1536]{1,0:T(8,128)S(1)}, f32[64,1536]{1,0:T(8,128)}, u32[]{:S(2)}) copy-start(f32[64,1536]{1,0:T(8,128)} %get-tuple-element.54) | copy-start | bytes 1179652
  112.4 14.4 %copy-start.15 = (f32[64,1024]{1,0:T(8,128)S(1)}, f32[64,1024]{1,0:T(8,128)}, u32[]{:S(2)}) copy-start(f32[64,1024]{1,0:T(8,128)} %get-tuple-element.100) | copy-start | bytes 786436
  113.3 11.3 %collective-permute-start.6 = (f32[64,128]{1,0:T(8,128)S(1)}, f32[64,128]{1,0:T(8,128)S(1)}, u32[]{:S(2)}, u32[]{:S(2)}) collective-permute-start(f32[64,128]{1,0:T(8,128)S(1)} %get-tuple-element.95), channel_id=1, source_target_pairs={{0,31},{1,0},{2,1},{3,2},{4,3},{5,4},{6,5},{7,6},{8,7},{9,8},{10,9... | collective-permute-start | bytes 98312 | tf_op jit(solution)/shard_map/ppermute | solution.py:17
  121.0 7.2 %copy-start.7 = (bf16[512,64]{0,1:T(8,128)(2,1)S(1)}, bf16[512,64]{0,1:T(8,128)(2,1)}, u32[]{:S(2)}) copy-start(bf16[512,64]{0,1:T(8,128)(2,1)} %param.21) | copy-start | bytes 196612
  121.0 4.9 %collective-permute-start.5 = (f32[64,128]{1,0:T(8,128)S(1)}, f32[64,128]{1,0:T(8,128)S(1)}, u32[]{:S(2)}, u32[]{:S(2)}) collective-permute-start(f32[64,128]{1,0:T(8,128)S(1)} %get-tuple-element.93), channel_id=1, source_target_pairs={{0,32},{32,64},{64,96},{96,128},{128,160},{160,192},{192,224},{224... | collective-permute-start | bytes 98312 | tf_op jit(solution)/shard_map/ppermute | solution.py:17
  121.0 5.3 %collective-permute-start.7 = (f32[64,128]{1,0:T(8,128)S(1)}, f32[64,128]{1,0:T(8,128)S(1)}, u32[]{:S(2)}, u32[]{:S(2)}) collective-permute-start(f32[64,128]{1,0:T(8,128)S(1)} %get-tuple-element.94), channel_id=1, source_target_pairs={{0,1},{1,2},{2,3},{3,4},{4,5},{5,6},{6,7},{7,8},{8,9},{9,10},{10,1... | collective-permute-start | bytes 98312 | tf_op jit(solution)/shard_map/ppermute | solution.py:17
  121.1 5.7 %collective-permute-start.4 = (f32[64,128]{1,0:T(8,128)S(1)}, f32[64,128]{1,0:T(8,128)S(1)}, u32[]{:S(2)}, u32[]{:S(2)}) collective-permute-start(f32[64,128]{1,0:T(8,128)S(1)} %get-tuple-element.92), channel_id=1, source_target_pairs={{0,224},{32,0},{64,32},{96,64},{128,96},{160,128},{192,160},{224,1... | collective-permute-start | bytes 98312 | tf_op jit(solution)/shard_map/ppermute | solution.py:17
  175.7 3.2 %copy-start.1 = (f32[512,512]{1,0:T(8,128)S(1)}, f32[512,512]{1,0:T(8,128)}, u32[]{:S(2)}) copy-start(f32[512,512]{1,0:T(8,128)} %get-tuple-element.192) | copy-start | bytes 3145732
  178.9 1.0 copy-start.6
  178.9 1.7 copy-start.5
  178.9 2.3 %copy-start.9 = (f32[16,64]{1,0:T(8,128)S(1)}, f32[16,64]{1,0:T(8,128)}, u32[]{:S(2)}) copy-start(f32[16,64]{1,0:T(8,128)} %get-tuple-element.195) | copy-start | bytes 12292

commit v2 on v1

v2 whole, which is shorter than its diff:
```python
import functools

import jax
import jax.numpy as jnp
from jax import lax
from jax.experimental import pallas as pl
from jax.experimental.pallas import tpu as pltpu
from jax.sharding import PartitionSpec as P

MESH = pl.DeviceIdType.MESH
DMA = pltpu.SemaphoreType.DMA


def where_am_i():
    slab, brick = lax.axis_index("slab"), lax.axis_index("brick")
    near = lax.rem(brick, 16)
    far = slab * 2 + brick // 16
    return slab, brick, near, far


def near_peer(step):
    slab, brick, near, _ = where_am_i()
    return slab, (brick // 16) * 16 + lax.rem(near + step, 16)


def far_peer(step):
    _, _, near, far = where_am_i()
    other = lax.rem(far + step, 16)
    return other // 2, lax.rem(other, 2) * 16 + near


def z_peer(step):
    slab, brick, near, _ = where_am_i()
    return slab, (brick // 16) * 16 + lax.rem(near + 2 * step, 16)


def core_peer():
    slab, brick, _, _ = where_am_i()
    return slab, brick + 1 - 2 * lax.rem(brick, 2)


def remote(source, target, send, recv, peer):
    return pltpu.make_async_remote_copy(
        src_ref=source, dst_ref=target, send_sem=send, recv_sem=recv,
        device_id=peer, device_id_type=MESH,
    )


def each(count, body):
    def step(index, carry):
        body(index)
        return carry

    lax.fori_loop(0, count, step, 0)


class Exchange:
    def __init__(self, count, source, target, sems, peer):
        self.count, self.source, self.target, self.sems, self.peer = count, source, target, sems, peer

    def copy(self, s):
        send, recv = self.sems
        return remote(self.source(s), self.target(s), send.at[s], recv.at[s], self.peer(s + 1))

    def start(self):
        each(self.count, lambda s: self.copy(s).start())

    def arrived(self):
        each(self.count, lambda s: self.copy(s).wait_recv())

    def sent(self):
        each(self.count, lambda s: self.copy(s).wait_send())


def small_stages(own, got, mid, last, sems):
    _, _, near, far = where_am_i()
    scatter = Exchange(
        15, lambda s: own.at[lax.rem(near + s + 1, 16)], lambda s: got.at[s], sems[0], near_peer
    )
    spread = Exchange(15, lambda s: mid.at[far], lambda s: mid.at[far], sems[1], far_peer)
    gather = Exchange(15, lambda s: last.at[near], lambda s: last.at[near], sems[2], near_peer)

    def middle():
        scatter.arrived()
        total = own[near]
        for s in range(15):
            total = total + got[s]
        mid[far] = total

    def final():
        spread.arrived()
        total = mid[0]
        for s in range(1, 16):
            total = total + mid[s]
        last[near] = total.astype(last.dtype)

    return scatter, middle, spread, final, gather


def announce():
    slab, brick, _, _ = where_am_i()
    barrier = pltpu.get_barrier_semaphore()

    def tell(peer):
        pl.semaphore_signal(barrier, inc=1, device_id=peer, device_id_type=MESH)

    each(15, lambda s: tell(near_peer(s + 1)))
    each(15, lambda s: tell(far_peer(s + 1)))
    tell((slab, lax.rem(brick + 1, 32)))
    tell((slab, lax.rem(brick + 31, 32)))
    return barrier


F32, BF16 = jnp.float32, jnp.bfloat16


def sigmoid(value):
    return 0.5 * jnp.tanh(0.5 * value) + 0.5


def silu_grad(value):
    sig = sigmoid(value)
    return sig * (1.0 + value * (1.0 - sig))


def dot(a, b, ca=1, cb=0):
    return lax.dot_general(a, b, (((ca,), (cb,)), ((), ())), preferred_element_type=F32)


def low_onehot(low):
    width = low.shape[1]
    positions = lax.broadcasted_iota(jnp.int32, (256, width), 0)
    return jnp.where(positions == low, 1.0, 0.0).astype(BF16)


def slice_of(s):
    return pl.ds(8 * (s // 2), 8), pl.ds(256 * (s % 2), 256)


def fused_kernel(
    embed, cot, basis, index, count, rows_out, w_res, w_down, w_up, w_basis,
    edge_out, res_out, down_out, up_out, basis_out,
    table, pre, ghost_send, ghost_hot, down_t, dres, res_sum, wts, dsum,
    hot, picked, tsum, dt, table_sum, back_send, back_got, dpre,
    own_d, got_d, mid_d, last_d, own_u, got_u, mid_u, last_u, basis_got, basis_mid,
    half_send, half_got, z_send, z_got, res_mid, res_last, res_other,
    sem_ghost, sem_back, sem_d, sem_u, sem_basis, sem_core, sem_z, sem_far,
):
    slab, brick, near, far = where_am_i()
    core, z = lax.rem(near, 2), near // 2
    ahead = ((lax.rem(slab + 1, 8), brick), (lax.rem(slab + 7, 8), brick),
             (slab, lax.rem(brick + 1, 32)), (slab, lax.rem(brick + 31, 32)))
    behind = (ahead[1], ahead[0], ahead[3], ahead[2])
    barrier = announce()

    down_t[...] = w_down[...].astype(F32).T.astype(BF16)
    pre_all = dot(down_t[...], embed[...], 1, 1)
    for c in range(4):
        part = pre_all[:, 256 * c : 256 * c + 256]
        pre[64 * c : 64 * c + 64, :] = part
        table[64 * c : 64 * c + 64, :] = (part * sigmoid(part)).astype(BF16)
    for k in range(4):
        sent = rows_out[k : k + 1, :]
        lanes = pl.ds(128 * k, 128)
        ghost_hot[:, lanes] = low_onehot(jnp.bitwise_and(sent, 255))
        wide = dot(table[0:256, :], ghost_hot[:, lanes])
        chunk = jnp.right_shift(sent, 8)
        chosen = wide[0:64]
        for c in range(1, 4):
            chosen = jnp.where(chunk == c, wide[64 * c : 64 * c + 64], chosen)
        ghost_send[k] = chosen.astype(BF16)
    pl.semaphore_wait(barrier, 32)

    def ghost_copy(k):
        place = table.at[pl.ds(256 + 64 * (k // 2), 64), pl.ds(128 * (k % 2), 128)]
        return remote(ghost_send.at[k], place, sem_ghost.at[0, k], sem_ghost.at[1, k], ahead[k])

    for k in range(4):
        ghost_copy(k).start()

    def residual(i):
        rows = pl.ds(pl.multiple_of(256 * i, 256), 256)
        value = dot(embed[rows, :], w_res[...])
        dres[rows, :] = (cot[rows, :].astype(F32) * silu_grad(value)).astype(BF16)

    each(4, residual)

    def residual_grad(i):
        rows = pl.ds(pl.multiple_of(128 * i, 128), 128)
        res_sum[rows, :] = dot(embed[:, rows], dres[...], 0, 0)

    each(4, residual_grad)
    other_half = pl.ds(pl.multiple_of((1 - core) * 256, 256), 256)
    half_send[...] = res_sum[other_half, :].astype(BF16)
    core_first = remote(half_send, half_got, sem_core.at[0], sem_core.at[1], core_peer())
    core_first.start()

    spread_n = (lax.broadcasted_iota(jnp.int32, (16, 256), 1) % 16) == lax.broadcasted_iota(jnp.int32, (16, 256), 0)
    wide_w = dot(w_basis[...], jnp.where(spread_n, 1.0, 0.0).astype(BF16), 0, 0)
    lane_slot = lax.broadcasted_iota(jnp.int32, (64, 256), 1) // 16
    for j in range(16):
        wts[j] = dot(jnp.where(lane_slot == j, wide_w, 0.0).astype(BF16), basis[...])
    dsum[...] = dot(w_up[...], cot[...], 1, 1)

    core_first.wait_recv()
    mine = pl.multiple_of(core * 256, 256)

    def to_z(t):
        rows = pl.ds(pl.multiple_of(mine + 32 * t, 32), 32)
        got = half_got[pl.ds(pl.multiple_of(32 * t, 32), 32), :]
        z_send[t] = (res_sum[rows, :] + got.astype(F32)).astype(BF16)

    each(8, to_z)
    z_scatter = Exchange(
        7, lambda s: z_send.at[lax.rem(z + s + 1, 8)], lambda s: z_got.at[s], (sem_z.at[0, 0], sem_z.at[1, 0]), z_peer
    )
    z_scatter.start()
    for k in range(4):
        ghost_copy(k).wait_recv()

    tsum[...] = jnp.zeros_like(tsum)

    def gather(j):
        row = index[pl.ds(j, 1), :]
        low = jnp.where(j < count[...], jnp.bitwise_and(row, 255), -1)
        chunk = jnp.right_shift(row, 8)
        hot[j] = low_onehot(low)
        wide = dot(table[...], hot[j])
        chosen = wide[0:64]
        for c in range(1, 6):
            chosen = jnp.where(chunk == c, wide[64 * c : 64 * c + 64], chosen)
        picked[j] = chosen.astype(BF16)
        tsum[...] += wts[j] * chosen

    each(16, gather)

    z_scatter.arrived()
    mine_z = pl.ds(pl.multiple_of(32 * z, 32), 32)
    part = res_sum[pl.ds(pl.multiple_of(mine + 32 * z, 32), 32), :] + half_got[mine_z, :].astype(F32)
    for s in range(7):
        part = part + z_got[s].astype(F32)
    res_mid[far] = part.astype(BF16)
    res_spread = Exchange(15, lambda s: res_mid.at[far], lambda s: res_mid.at[far], (sem_far.at[0], sem_far.at[1]), far_peer)
    res_spread.start()

    total = tsum[...]
    act = (total * sigmoid(total)).astype(BF16)
    dt[...] = dsum[...] * silu_grad(total)
    up_grad = dot(act, cot[...])
    for s in range(16):
        own_u[s] = up_grad[8 * (s // 2) : 8 * (s // 2) + 8, 256 * (s % 2) : 256 * (s % 2) + 256]
    sems_u = [(sem_u.at[0, t], sem_u.at[1, t]) for t in range(3)]
    scatter_u, middle_u, spread_u, final_u, gather_u = small_stages(own_u, got_u, mid_u, last_u, sems_u)
    scatter_u.start()

    table_sum[...] = jnp.zeros_like(table_sum)

    def scatter(j):
        chunk = jnp.right_shift(index[pl.ds(j, 1), :], 8)
        slope = dt[...]
        term = (slope * wts[j]).astype(BF16)
        picked[j] = (slope * picked[j].astype(F32)).astype(BF16)
        parts = [term * jnp.where(chunk == c, 1.0, 0.0).astype(BF16) for c in range(6)]
        table_sum[...] += dot(jnp.concatenate(parts, axis=0), hot[j], 1, 1)

    each(16, scatter)

    def back_copy(k):
        return remote(back_send.at[k], back_got.at[k], sem_back.at[0, k], sem_back.at[1, k], behind[k])

    for k in range(4):
        back_send[k] = table_sum[256 + 64 * (k // 2) : 320 + 64 * (k // 2), 128 * (k % 2) : 128 * (k % 2) + 128].astype(BF16)
        back_copy(k).start()

    basis_grad = jnp.zeros((16, 64), F32)
    for j in range(16):
        basis_grad = basis_grad + dot(basis[16 * j : 16 * j + 16, :], picked[j], 1, 1)
    basis_got[near] = basis_grad
    basis_a = Exchange(15, lambda s: basis_got.at[near], lambda s: basis_got.at[near], (sem_basis.at[0, 0], sem_basis.at[1, 0]), near_peer)
    basis_a.start()

    middle_u()
    spread_u.start()
    res_spread.arrived()
    part = res_mid[0].astype(F32)
    for s in range(1, 16):
        part = part + res_mid[s].astype(F32)
    res_last[mine_z, :] = part.astype(BF16)
    z_gather = Exchange(7, lambda s: res_last.at[mine_z, :], lambda s: res_last.at[mine_z, :], (sem_z.at[0, 1], sem_z.at[1, 1]), z_peer)
    z_gather.start()

    for k in range(4):
        back_copy(k).wait_recv()
    returned = table_sum[0:256, :]
    for k in range(4):
        chunk = jnp.right_shift(rows_out[k : k + 1, :], 8)
        term = back_got[k]
        parts = [term * jnp.where(chunk == c, 1.0, 0.0).astype(BF16) for c in range(4)]
        returned = returned + dot(jnp.concatenate(parts, axis=0), ghost_hot[:, 128 * k : 128 * k + 128], 1, 1)
    returned = (returned * silu_grad(pre[...])).astype(BF16)
    for c in range(4):
        dpre[:, 256 * c : 256 * c + 256] = returned[64 * c : 64 * c + 64, :]
    down_grad = dot(dpre[...], embed[...])
    for s in range(16):
        own_d[s] = down_grad[8 * (s // 2) : 8 * (s // 2) + 8, 256 * (s % 2) : 256 * (s % 2) + 256]
    sems_d = [(sem_d.at[0, t], sem_d.at[1, t]) for t in range(3)]
    scatter_d, middle_d, spread_d, final_d, gather_d = small_stages(own_d, got_d, mid_d, last_d, sems_d)
    scatter_d.start()

    basis_a.arrived()
    basis_total = basis_got[0]
    for s in range(1, 16):
        basis_total = basis_total + basis_got[s]
    basis_mid[far] = basis_total
    basis_b = Exchange(15, lambda s: basis_mid.at[far], lambda s: basis_mid.at[far], (sem_basis.at[0, 1], sem_basis.at[1, 1]), far_peer)
    basis_b.start()

    def edge(i):
        rows = pl.ds(pl.multiple_of(256 * i, 256), 256)
        value = dot(dres[rows, :], w_res[...], 1, 1) + dot(dpre[:, rows], down_t[...], 0, 0)
        edge_out[rows, :] = value.astype(BF16)

    each(4, edge)

    middle_d()
    spread_d.start()
    final_u()
    gather_u.start()
    z_gather.arrived()
    core_last = remote(res_last, res_other, sem_core.at[2], sem_core.at[3], core_peer())
    core_last.start()
    res_out[pl.ds(mine, 256), :] = res_last[...].astype(F32)
    final_d()
    gather_d.start()
    basis_b.arrived()
    basis_total = basis_mid[0]
    for s in range(1, 16):
        basis_total = basis_total + basis_mid[s]
    basis_out[...] = basis_total
    gather_u.arrived()
    for s in range(16):
        up_out[8 * (s // 2) : 8 * (s // 2) + 8, 256 * (s % 2) : 256 * (s % 2) + 256] = last_u[s].astype(F32)
    core_last.wait_recv()
    res_out[other_half, :] = res_other[...].astype(F32)
    for k in range(4):
        ghost_copy(k).wait_send()
        back_copy(k).wait_send()
    for exchange in (scatter_u, spread_u, gather_u, scatter_d, spread_d, basis_a, basis_b, z_scatter, res_spread, z_gather):
        exchange.sent()
    core_first.wait_send()
    core_last.wait_send()
    gather_d.arrived()
    for r in range(8):
        block = jnp.concatenate([last_d[2 * r], last_d[2 * r + 1]], axis=1)
        dpre[8 * r : 8 * r + 8, 0:512] = block
    down_out[...] = dpre[:, 0:512].astype(F32).T
    gather_d.sent()


def shards(
    embed, cotangent, basis, triplet_row_index, triplet_slot_count, outgoing_edge_rows,
    residual_weight, down_weight, up_weight, basis_weight,
):
    vmem = pltpu.VMEM
    return pl.pallas_call(
        fused_kernel,
        out_shape=(
            jax.ShapeDtypeStruct((1024, 512), BF16),
            jax.ShapeDtypeStruct((512, 512), F32),
            jax.ShapeDtypeStruct((512, 64), F32),
            jax.ShapeDtypeStruct((64, 512), F32),
            jax.ShapeDtypeStruct((16, 64), F32),
        ),
        in_specs=[pl.BlockSpec(memory_space=vmem)] * 10,
        out_specs=[pl.BlockSpec(memory_space=vmem)] * 5,
        scratch_shapes=[
            vmem((384, 256), BF16),
            vmem((256, 256), F32),
            vmem((4, 64, 128), BF16),
            vmem((256, 512), BF16),
            vmem((64, 512), BF16),
            vmem((1024, 512), BF16),
            vmem((512, 512), F32),
            vmem((16, 64, 1024), F32),
            vmem((64, 1024), F32),
            vmem((16, 256, 1024), BF16),
            vmem((16, 64, 1024), BF16),
            vmem((64, 1024), F32),
            vmem((64, 1024), F32),
            vmem((384, 256), F32),
            vmem((4, 64, 128), BF16),
            vmem((4, 64, 128), BF16),
            vmem((64, 1024), BF16),
            vmem((16, 8, 256), F32),
            vmem((15, 8, 256), F32),
            vmem((16, 8, 256), F32),
            vmem((16, 8, 256), BF16),
            vmem((16, 8, 256), F32),
            vmem((15, 8, 256), F32),
            vmem((16, 8, 256), F32),
            vmem((16, 8, 256), BF16),
            vmem((16, 16, 64), F32),
            vmem((16, 16, 64), F32),
            vmem((256, 512), BF16),
            vmem((256, 512), BF16),
            vmem((8, 32, 512), BF16),
            vmem((7, 32, 512), BF16),
            vmem((16, 32, 512), BF16),
            vmem((256, 512), BF16),
            vmem((256, 512), BF16),
            DMA((2, 4)),
            DMA((2, 4)),
            DMA((2, 3, 15)),
            DMA((2, 3, 15)),
            DMA((2, 2, 15)),
            DMA((4,)),
            DMA((2, 2, 7)),
            DMA((2, 15)),
        ],
        compiler_params=pltpu.CompilerParams(
            collective_id=0, has_side_effects=True, vmem_limit_bytes=60 * 1024 * 1024
        ),
        name="fused",
    )(
        embed, cotangent, basis.reshape(256, 1024), triplet_row_index, triplet_slot_count.reshape(1, 1024),
        outgoing_edge_rows, residual_weight, down_weight, up_weight, basis_weight,
    )


def solution(mesh):
    in_specs = (
        P(("slab", "brick"), None),
        P(("slab", "brick"), None),
        P(None, None, ("slab", "brick")),
        P(None, ("slab", "brick")),
        P(("slab", "brick")),
        P(None, ("slab", "brick")),
        P(),
        P(),
        P(),
        P(),
    )
    out_specs = (P(("slab", "brick"), None), P(), P(), P(), P())
    return jax.shard_map(shards, mesh=mesh, in_specs=in_specs, out_specs=out_specs, check_vma=False)
```

time: 185 us -> 71.8 us (0.39); the launches traced: 182 us -> 71.5 us
  matrix products: 85.6 us -> 0 us
  local copies, waits for them, and re-layouts: 29.7 us -> 7.99 us
  starting transfers between devices: 16.7 us -> 0 us
  Pallas kernels: 47 us -> 62.9 us
    dot_general x50 -> x0, matrix products: 85.6 us -> none  [the longest x16 48.6 us: scatter_slot(): lax.dot_general(slot_terms.astype(jnp.bfloat16), onehot, (((1,), (1,)), (...]
    dynamic_slice x32 -> x0, local copies, waits for them, and re-layouts: 24.5 us -> none  [shards(): lax.scan(gather_slot, jnp.zeros((), jnp.float32), triplet_row_index)]
    ppermute x8 -> x0, starting transfers between devices: 16.7 us -> none  [passed_along(): return lax.ppermute(value, axis, pairs)]
    pallas_call x1, Pallas kernels: 47 us -> 62.9 us  [shards(): pl.pallas_call(fused_kernel, out_shape=(jax.ShapeDtypeStruct((1024, 512),...]
    unnamed x39 -> x11, local copies, waits for them, and re-layouts: 3.38 us -> 6.27 us
  transfers between devices with their start and end apart: 8 -> 0, of which waited for: 1 -> 0; matrix products, arithmetic and copies ran while one was open for 4% -> 0% of each run, Pallas kernels for 0% -> 0%
where the time goes in v2:
time: 71.8 us; the launch traced here: 71.5 us
  Pallas kernels  62.9 us (88%)
  local copies, waits for them, and re-layouts  7.99 us (11%)
    pallas_call x1, Pallas kernels, shards(): pl.pallas_call(fused_kernel, out_shape=(jax.ShapeDtypeStruct((1024, 512),...  62.9 us
    unnamed x11, local copies, waits for them, and re-layouts  6.27 us
    pallas_call x1, local copies, waits for them, and re-layouts, shards(): pl.pallas_call(fused_kernel, out_shape=(jax.ShapeDtypeStruct((1024, 512),...  1.72 us

profile of v2, /device:TPU:1, one launch (start us, length us, event | category | flops | bytes accessed | tf_op | source)
XLA Modules:
  0.0 71.5 jit_solution(11440231328857331875)
XLA Ops:
  0.6 1.6 %copy.15.w_down = bf16[512,64]{1,0:T(8,128)(2,1)} copy(bf16[512,64]{0,1:T(8,128)(2,1)} %param.17) | data formatting | bytes 131072 | tf_op args[7]
  2.2 62.9 %fused.1 = (bf16[1024,512]{1,0:T(8,128)(2,1)}, f32[512,512]{1,0:T(8,128)}, f32[512,64]{1,0:T(8,128)}, f32[64,512]{1,0:T(8,128)}, f32[16,64]{1,0:T(8,128)}) custom-call(bf16[1024,512]{1,0:T(8,128)(2,1)} %embed.1, bf16[1024,512]{1,0:T(8,128)(2,1)} %cot.1, bf16[256,1024]{1,0:T(8,128)(2,1)} %bitcast.2, s32[16,1024]{1,0:T(8,128)} %index.1, s32[1,1024]{1,0:T(1,128)} %bitcast.3, ...), custom_call_target="tpu_custom_call" | custom-call | tf_op jit(solution)/shard_map/fused/pallas_call | solution.py:365
  65.1 1.7 %copy.16 = f32[512,64]{0,1:T(8,128)} copy(f32[512,64]{1,0:T(8,128)} %get-tuple-element.7) | data formatting | bytes 262144 | tf_op jit(solution)/shard_map/fused/pallas_call | solution.py:365
  66.9 0.0 copy-start
  66.9 2.4 %copy.21 = bf16[1024,512]{1,0:T(8,128)(2,1)} copy(bf16[1024,512]{1,0:T(8,128)(2,1)} %get-tuple-element.15) | data formatting | bytes 2097152
  69.2 0.0 copy-done
  69.2 0.0 copy-start.1
  69.2 1.0 %copy.22 = f32[512,512]{1,0:T(8,128)} copy(f32[512,512]{1,0:T(8,128)S(1)} %copy-done) | data formatting | bytes 2097152
  70.2 0.1 copy-done.1
  70.2 0.0 copy-start.2
  70.2 0.7 copy.23
  70.9 0.0 copy-done.2
  70.9 0.6 copy.24
Async XLA Ops:
  66.9 2.4 %copy-start = (f32[512,512]{1,0:T(8,128)S(1)}, f32[512,512]{1,0:T(8,128)}, u32[]{:S(2)}) copy-start(f32[512,512]{1,0:T(8,128)} %get-tuple-element.16) | copy-start | bytes 3145732
  69.2 1.0 %copy-start.1 = (f32[64,512]{1,0:T(8,128)S(1)}, f32[64,512]{1,0:T(8,128)}, u32[]{:S(2)}) copy-start(f32[64,512]{1,0:T(8,128)} %get-tuple-element.18) | copy-start | bytes 393220
  70.2 0.7 copy-start.2

commit v3 on v2

v3 whole, which is shorter than its diff:
```python
import functools

import jax
import jax.numpy as jnp
from jax import lax
from jax.experimental import pallas as pl
from jax.experimental.pallas import tpu as pltpu
from jax.sharding import PartitionSpec as P

MESH = pl.DeviceIdType.MESH
DMA = pltpu.SemaphoreType.DMA


def where_am_i():
    slab, brick = lax.axis_index("slab"), lax.axis_index("brick")
    near = lax.rem(brick, 16)
    far = slab * 2 + brick // 16
    return slab, brick, near, far


def near_peer(step):
    slab, brick, near, _ = where_am_i()
    return slab, (brick // 16) * 16 + lax.rem(near + step, 16)


def far_peer(step):
    _, _, near, far = where_am_i()
    other = lax.rem(far + step, 16)
    return other // 2, lax.rem(other, 2) * 16 + near


def z_peer(step):
    slab, brick, near, _ = where_am_i()
    return slab, (brick // 16) * 16 + lax.rem(near + 2 * step, 16)


def core_peer():
    slab, brick, _, _ = where_am_i()
    return slab, brick + 1 - 2 * lax.rem(brick, 2)


def remote(source, target, send, recv, peer):
    return pltpu.make_async_remote_copy(
        src_ref=source, dst_ref=target, send_sem=send, recv_sem=recv,
        device_id=peer, device_id_type=MESH,
    )


def each(count, body, unroll=1):
    def step(index, carry):
        body(index)
        return carry

    lax.fori_loop(0, count, step, 0, unroll=unroll)


class Exchange:
    def __init__(self, count, source, target, gone, came, sems, peer):
        self.count, self.source, self.target, self.gone, self.came = count, source, target, gone, came
        self.sems, self.peer = sems, peer

    def start(self):
        send, recv = self.sems
        each(self.count, lambda s: remote(self.source(s), self.target(s), send, recv, self.peer(s + 1)).start())

    def arrived(self):
        pltpu.make_async_copy(self.came, self.came, self.sems[1]).wait()

    def sent(self):
        pltpu.make_async_copy(self.gone, self.gone, self.sems[0]).wait()


def small_stages(own, got, mid, last, sems):
    _, _, near, far = where_am_i()
    scatter = Exchange(
        15, lambda s: own.at[lax.rem(far + s + 1, 16)], lambda s: got.at[s], got, got, sems[0], far_peer
    )
    spread = Exchange(15, lambda s: mid.at[near], lambda s: mid.at[near], mid.at[0:15], mid.at[0:15], sems[1], near_peer)
    gather = Exchange(15, lambda s: last.at[far], lambda s: last.at[far], last.at[0:15], last.at[0:15], sems[2], far_peer)

    def middle():
        scatter.arrived()
        total = own[far]
        for s in range(15):
            total = total + got[s]
        mid[near] = total

    def final():
        spread.arrived()
        total = mid[0]
        for s in range(1, 16):
            total = total + mid[s]
        last[far] = total.astype(last.dtype)

    return scatter, middle, spread, final, gather


def announce():
    slab, brick, _, _ = where_am_i()
    barrier = pltpu.get_barrier_semaphore()

    def tell(peer):
        pl.semaphore_signal(barrier, inc=1, device_id=peer, device_id_type=MESH)

    each(15, lambda s: tell(near_peer(s + 1)))
    each(15, lambda s: tell(far_peer(s + 1)))
    tell((slab, lax.rem(brick + 1, 32)))
    tell((slab, lax.rem(brick + 31, 32)))
    return barrier


F32, BF16 = jnp.float32, jnp.bfloat16


def sigmoid(value):
    return 0.5 * jnp.tanh(0.5 * value) + 0.5


def silu_grad(value):
    sig = sigmoid(value)
    return sig * (1.0 + value * (1.0 - sig))


def dot(a, b, ca=1, cb=0):
    return lax.dot_general(a, b, (((ca,), (cb,)), ((), ())), preferred_element_type=F32)


def low_onehot(low):
    width = low.shape[1]
    positions = lax.broadcasted_iota(jnp.int32, (256, width), 0)
    return jnp.where(positions == low, 1.0, 0.0).astype(BF16)


def slice_of(s):
    return pl.ds(8 * (s // 2), 8), pl.ds(256 * (s % 2), 256)


def fused_kernel(
    embed_hbm, cot_hbm, basis_hbm, index_hbm, count_hbm, rows_hbm, w_res_hbm, down_hbm, w_up_hbm, w_basis_hbm,
    edge_hbm, res_hbm, small_out,
    embed, cot, basis, index, count, rows_out, w_res, down_t, w_up, w_basis,
    table, pre, ghost_send, ghost_hot, dres, res_sum, wts, dsum,
    hot, picked, tsum, dt, table_sum, back_send, back_got, dpre,
    own_d, got_d, mid_d, last_d, own_u, got_u, mid_u, last_u, basis_got, basis_mid,
    half_send, half_got, far_send, far_got, res_mid, res_last, res_other,
    sem_ghost, sem_back, sem_d, sem_u, sem_basis, sem_core, sem_z, sem_far, sem_in, sem_out, edge_out, res_out,
):
    slab, brick, near, far = where_am_i()
    core, z = lax.rem(near, 2), near // 2
    ahead = ((lax.rem(slab + 1, 8), brick), (lax.rem(slab + 7, 8), brick),
             (slab, lax.rem(brick + 1, 32)), (slab, lax.rem(brick + 31, 32)))
    behind = (ahead[1], ahead[0], ahead[3], ahead[2])
    loads = {}
    for place, (name, source, target) in enumerate((
        ("embed", embed_hbm, embed), ("down", down_hbm, down_t), ("rows", rows_hbm, rows_out), ("w_res", w_res_hbm, w_res),
        ("cot", cot_hbm, cot), ("basis", basis_hbm, basis), ("w_basis", w_basis_hbm, w_basis), ("w_up", w_up_hbm, w_up),
        ("index", index_hbm, index), ("count", count_hbm, count),
    )):
        loads[name] = pltpu.make_async_copy(source, target, sem_in.at[place])
    for name in ("embed", "down", "rows"):
        loads[name].start()
    barrier = announce()
    for name in ("w_res", "cot", "basis", "w_basis", "w_up", "index", "count"):
        loads[name].start()

    loads["down"].wait()
    loads["embed"].wait()
    pre_all = dot(down_t[...], embed[...], 1, 1)
    for c in range(4):
        part = pre_all[:, 256 * c : 256 * c + 256]
        pre[64 * c : 64 * c + 64, :] = part
        table[64 * c : 64 * c + 64, :] = (part * sigmoid(part)).astype(BF16)
    loads["rows"].wait()
    for k in range(4):
        sent = rows_out[k : k + 1, :]
        lanes = pl.ds(128 * k, 128)
        ghost_hot[:, lanes] = low_onehot(jnp.bitwise_and(sent, 255))
        wide = dot(table[0:256, :], ghost_hot[:, lanes])
        chunk = jnp.right_shift(sent, 8)
        chosen = wide[0:64]
        for c in range(1, 4):
            chosen = jnp.where(chunk == c, wide[64 * c : 64 * c + 64], chosen)
        ghost_send[k] = chosen.astype(BF16)
    loads["w_res"].wait()
    loads["cot"].wait()

    def residual(i):
        rows = pl.ds(pl.multiple_of(256 * i, 256), 256)
        value = dot(embed[rows, :], w_res[...])
        dres[rows, :] = (cot[rows, :].astype(F32) * silu_grad(value)).astype(BF16)

    each(4, residual)

    def residual_grad(i):
        rows = pl.ds(pl.multiple_of(128 * i, 128), 128)
        res_sum[rows, :] = dot(embed[:, rows], dres[...], 0, 0)

    each(4, residual_grad)
    other_half = pl.ds(pl.multiple_of((1 - core) * 256, 256), 256)
    half_send[...] = res_sum[other_half, :].astype(BF16)
    pl.semaphore_wait(barrier, 32)

    def ghost_copy(k):
        place = table.at[pl.ds(256 + 64 * (k // 2), 64), pl.ds(128 * (k % 2), 128)]
        return remote(ghost_send.at[k], place, sem_ghost.at[0], sem_ghost.at[1], ahead[k])

    for k in range(4):
        ghost_copy(k).start()

    core_first = remote(half_send, half_got, sem_core.at[0], sem_core.at[1], core_peer())
    core_first.start()

    for name in ("basis", "w_basis", "w_up", "index", "count"):
        loads[name].wait()
    spread_n = (lax.broadcasted_iota(jnp.int32, (16, 256), 1) % 16) == lax.broadcasted_iota(jnp.int32, (16, 256), 0)
    wide_w = dot(w_basis[...], jnp.where(spread_n, 1.0, 0.0).astype(BF16), 0, 0)
    lane_slot = lax.broadcasted_iota(jnp.int32, (64, 256), 1) // 16
    for j in range(16):
        wts[j] = dot(jnp.where(lane_slot == j, wide_w, 0.0).astype(BF16), basis[...])
    dsum[...] = dot(w_up[...], cot[...], 1, 1)

    core_first.wait_recv()
    mine = pl.multiple_of(core * 256, 256)

    def to_far(t):
        rows = pl.ds(pl.multiple_of(mine + 16 * t, 16), 16)
        got = half_got[pl.ds(pl.multiple_of(16 * t, 16), 16), :]
        far_send[t] = (res_sum[rows, :] + got.astype(F32)).astype(BF16)

    each(16, to_far)
    res_scatter = Exchange(
        15, lambda s: far_send.at[lax.rem(far + s + 1, 16)], lambda s: far_got.at[s], far_got, far_got, (sem_far.at[0, 0], sem_far.at[1, 0]), far_peer
    )
    res_scatter.start()
    pltpu.make_async_copy(ghost_send, ghost_send, sem_ghost.at[1]).wait()

    tsum[...] = jnp.zeros_like(tsum)

    def gather(j):
        row = index[pl.ds(j, 1), :]
        low = jnp.where(j < count[...], jnp.bitwise_and(row, 255), -1)
        chunk = jnp.right_shift(row, 8)
        hot[j] = low_onehot(low)
        wide = dot(table[...], hot[j])
        chosen = wide[0:64]
        for c in range(1, 6):
            chosen = jnp.where(chunk == c, wide[64 * c : 64 * c + 64], chosen)
        picked[j] = chosen.astype(BF16)
        tsum[...] += wts[j] * chosen

    each(16, gather, 2)

    total = tsum[...]
    act = (total * sigmoid(total)).astype(BF16)
    dt[...] = dsum[...] * silu_grad(total)
    up_grad = dot(act, cot[...])
    for s in range(16):
        own_u[s] = up_grad[8 * (s // 2) : 8 * (s // 2) + 8, 256 * (s % 2) : 256 * (s % 2) + 256]
    sems_u = [(sem_u.at[0, t], sem_u.at[1, t]) for t in range(3)]
    scatter_u, middle_u, spread_u, final_u, gather_u = small_stages(own_u, got_u, mid_u, last_u, sems_u)
    scatter_u.start()

    table_sum[...] = jnp.zeros_like(table_sum)

    def scatter(j):
        chunk = jnp.right_shift(index[pl.ds(j, 1), :], 8)
        slope = dt[...]
        term = (slope * wts[j]).astype(BF16)
        picked[j] = (slope * picked[j].astype(F32)).astype(BF16)
        parts = [term * jnp.where(chunk == c, 1.0, 0.0).astype(BF16) for c in range(6)]
        table_sum[...] += dot(jnp.concatenate(parts, axis=0), hot[j], 1, 1)

    each(8, scatter, 2)
    res_scatter.arrived()
    mine_far = pl.ds(pl.multiple_of(16 * far, 16), 16)
    part = res_sum[pl.ds(pl.multiple_of(mine + 16 * far, 16), 16), :] + half_got[mine_far, :].astype(F32)
    for s in range(15):
        part = part + far_got[s].astype(F32)
    res_mid[z] = part.astype(BF16)
    res_spread = Exchange(7, lambda s: res_mid.at[z], lambda s: res_mid.at[z], res_mid.at[0:7], res_mid.at[0:7], (sem_z.at[0], sem_z.at[1]), z_peer)
    res_spread.start()
    each(8, lambda j: scatter(j + 8), 2)

    def back_copy(k):
        return remote(back_send.at[k], back_got.at[k], sem_back.at[0], sem_back.at[1], behind[k])

    for k in range(4):
        back_send[k] = table_sum[256 + 64 * (k // 2) : 320 + 64 * (k // 2), 128 * (k % 2) : 128 * (k % 2) + 128].astype(BF16)
        back_copy(k).start()

    basis_grad = jnp.zeros((16, 64), F32)
    for j in range(16):
        basis_grad = basis_grad + dot(basis[16 * j : 16 * j + 16, :], picked[j], 1, 1)
    basis_got[near] = basis_grad
    basis_a = Exchange(15, lambda s: basis_got.at[near], lambda s: basis_got.at[near], basis_got.at[0:15], basis_got.at[0:15], (sem_basis.at[0, 0], sem_basis.at[1, 0]), near_peer)
    basis_a.start()

    middle_u()
    spread_u.start()
    res_spread.arrived()
    part = res_mid[0].astype(F32)
    for s in range(1, 8):
        part = part + res_mid[s].astype(F32)
    res_last[mine_far, :] = part.astype(BF16)
    res_gather = Exchange(
        15, lambda s: res_last.at[mine_far, :], lambda s: res_last.at[mine_far, :], res_last.at[0:240], res_last.at[0:240], (sem_far.at[0, 1], sem_far.at[1, 1]), far_peer
    )
    res_gather.start()

    pltpu.make_async_copy(back_got, back_got, sem_back.at[1]).wait()
    returned = table_sum[0:256, :]
    for k in range(4):
        chunk = jnp.right_shift(rows_out[k : k + 1, :], 8)
        term = back_got[k]
        parts = [term * jnp.where(chunk == c, 1.0, 0.0).astype(BF16) for c in range(4)]
        returned = returned + dot(jnp.concatenate(parts, axis=0), ghost_hot[:, 128 * k : 128 * k + 128], 1, 1)
    returned = (returned * silu_grad(pre[...])).astype(BF16)
    for c in range(4):
        dpre[:, 256 * c : 256 * c + 256] = returned[64 * c : 64 * c + 64, :]
    down_grad = dot(dpre[...], embed[...])
    for s in range(16):
        own_d[s] = down_grad[8 * (s // 2) : 8 * (s // 2) + 8, 256 * (s % 2) : 256 * (s % 2) + 256]
    sems_d = [(sem_d.at[0, t], sem_d.at[1, t]) for t in range(3)]
    scatter_d, middle_d, spread_d, final_d, gather_d = small_stages(own_d, got_d, mid_d, last_d, sems_d)
    scatter_d.start()

    def edge(i):
        rows = pl.ds(pl.multiple_of(256 * i, 256), 256)
        value = dot(dres[rows, :], w_res[...], 1, 1) + dot(dpre[:, rows], down_t[...], 0, 0)
        edge_out[rows, :] = value.astype(BF16)

    each(4, edge)
    edge_copy = pltpu.make_async_copy(edge_out, edge_hbm, sem_out.at[0])
    edge_copy.start()

    basis_a.arrived()
    basis_total = basis_got[0]
    for s in range(1, 16):
        basis_total = basis_total + basis_got[s]
    basis_mid[far] = basis_total
    basis_b = Exchange(15, lambda s: basis_mid.at[far], lambda s: basis_mid.at[far], basis_mid.at[0:15], basis_mid.at[0:15], (sem_basis.at[0, 1], sem_basis.at[1, 1]), far_peer)
    basis_b.start()

    middle_d()
    spread_d.start()
    final_u()
    gather_u.start()
    res_gather.arrived()
    core_last = remote(res_last, res_other, sem_core.at[2], sem_core.at[3], core_peer())
    core_last.start()
    res_out[pl.ds(mine, 256), :] = res_last[...]
    final_d()
    gather_d.start()
    basis_b.arrived()
    basis_total = basis_mid[0]
    for s in range(1, 16):
        basis_total = basis_total + basis_mid[s]
    small_out[128:144, 0:64] = basis_total
    gather_u.arrived()
    for s in range(16):
        small_out[64 + 8 * (s // 2) : 72 + 8 * (s // 2), 256 * (s % 2) : 256 * (s % 2) + 256] = last_u[s].astype(F32)
    core_last.wait_recv()
    res_out[other_half, :] = res_other[...]
    res_copy = pltpu.make_async_copy(res_out, res_hbm, sem_out.at[1])
    res_copy.start()
    pltpu.make_async_copy(ghost_send, ghost_send, sem_ghost.at[0]).wait()
    pltpu.make_async_copy(back_send, back_send, sem_back.at[0]).wait()
    for exchange in (scatter_u, spread_u, gather_u, scatter_d, spread_d, basis_a, basis_b, res_scatter, res_spread, res_gather):
        exchange.sent()
    core_first.wait_send()
    core_last.wait_send()
    gather_d.arrived()
    for s in range(16):
        small_out[8 * (s // 2) : 8 * (s // 2) + 8, 256 * (s % 2) : 256 * (s % 2) + 256] = last_d[s].astype(F32)
    gather_d.sent()
    edge_copy.wait()
    res_copy.wait()


def copy_kernel(edge, res, small, edge_out, res_out, down_out, up_out, basis_out):
    edge_out[...] = edge[...]
    res_out[...] = res[...].astype(F32)
    down_out[...] = small[0:64, :]
    up_out[...] = small[64:128, :]
    basis_out[...] = small[128:144, 0:64]


def hand_over(edge, res, small):
    shapes = (((1024, 512), BF16), ((512, 512), F32), ((64, 512), F32), ((64, 512), F32), ((16, 64), F32))
    return pl.pallas_call(
        copy_kernel,
        out_shape=tuple(jax.ShapeDtypeStruct(*shape) for shape in shapes),
        in_specs=[pl.BlockSpec(memory_space=pltpu.VMEM)] * 3,
        out_specs=[pl.BlockSpec(memory_space=pltpu.VMEM)] * 5,
        compiler_params=pltpu.CompilerParams(vmem_limit_bytes=8 * 1024 * 1024),
        name="hand_over",
    )(edge, res, small)


def shards(
    embed, cotangent, basis, triplet_row_index, triplet_slot_count, outgoing_edge_rows,
    residual_weight, down_weight, up_weight, basis_weight,
):
    vmem = pltpu.VMEM
    edge, res, small = pl.pallas_call(
        fused_kernel,
        out_shape=(
            vmem((1024, 512), BF16),
            vmem((512, 512), BF16),
            vmem((144, 512), F32),
        ),
        in_specs=[pl.BlockSpec(memory_space=pltpu.HBM)] * 10,
        out_specs=[pl.BlockSpec(memory_space=pl.ANY), pl.BlockSpec(memory_space=pl.ANY), pl.BlockSpec(memory_space=vmem)],
        scratch_shapes=[
            vmem((1024, 512), BF16),
            vmem((1024, 512), BF16),
            vmem((256, 1024), BF16),
            vmem((16, 1024), jnp.int32),
            vmem((1, 1024), jnp.int32),
            vmem((4, 128), jnp.int32),
            vmem((512, 512), BF16),
            vmem((64, 512), BF16),
            vmem((64, 512), BF16),
            vmem((16, 64), BF16),
            vmem((384, 256), BF16),
            vmem((256, 256), F32),
            vmem((4, 64, 128), BF16),
            vmem((256, 512), BF16),
            vmem((1024, 512), BF16),
            vmem((512, 512), F32),
            vmem((16, 64, 1024), F32),
            vmem((64, 1024), F32),
            vmem((16, 256, 1024), BF16),
            vmem((16, 64, 1024), BF16),
            vmem((64, 1024), F32),
            vmem((64, 1024), F32),
            vmem((384, 256), F32),
            vmem((4, 64, 128), BF16),
            vmem((4, 64, 128), BF16),
            vmem((64, 1024), BF16),
            vmem((16, 8, 256), F32),
            vmem((15, 8, 256), F32),
            vmem((16, 8, 256), F32),
            vmem((16, 8, 256), BF16),
            vmem((16, 8, 256), F32),
            vmem((15, 8, 256), F32),
            vmem((16, 8, 256), F32),
            vmem((16, 8, 256), BF16),
            vmem((16, 16, 64), F32),
            vmem((16, 16, 64), F32),
            vmem((256, 512), BF16),
            vmem((256, 512), BF16),
            vmem((16, 16, 512), BF16),
            vmem((15, 16, 512), BF16),
            vmem((8, 16, 512), BF16),
            vmem((256, 512), BF16),
            vmem((256, 512), BF16),
            DMA((2,)),
            DMA((2,)),
            DMA((2, 3)),
            DMA((2, 3)),
            DMA((2, 2)),
            DMA((4,)),
            DMA((2,)),
            DMA((2, 2)),
            DMA((10,)),
            DMA((2,)),
            vmem((1024, 512), BF16),
            vmem((512, 512), BF16),
        ],
        compiler_params=pltpu.CompilerParams(
            collective_id=0, has_side_effects=True, vmem_limit_bytes=40 * 1024 * 1024
        ),
        name="fused",
    )(
        *(
            pltpu.with_memory_space_constraint(value, pltpu.HBM)
            for value in (
                embed, cotangent, basis.reshape(256, 1024), triplet_row_index, triplet_slot_count.reshape(1, 1024),
                outgoing_edge_rows, residual_weight, down_weight.T, up_weight, basis_weight,
            )
        )
    )
    edge, res, down, up, base = hand_over(edge, res, small)
    return edge, res, down.T, up, base


def solution(mesh):
    in_specs = (
        P(("slab", "brick"), None),
        P(("slab", "brick"), None),
        P(None, None, ("slab", "brick")),
        P(None, ("slab", "brick")),
        P(("slab", "brick")),
        P(None, ("slab", "brick")),
        P(),
        P(),
        P(),
        P(),
    )
    out_specs = (P(("slab", "brick"), None), P(), P(), P(), P())
    return jax.shard_map(shards, mesh=mesh, in_specs=in_specs, out_specs=out_specs, check_vma=False)
```

time: 71.8 us -> 51.7 us (0.72)
  Pallas kernels: 62.9 us -> 50.9 us
  local copies, waits for them, and re-layouts: 7.99 us -> 0 us
    pallas_call x1 -> x2, Pallas kernels: 62.9 us -> 50.9 us  [the longest x1 49.4 us: shards(): pl.pallas_call(fused_kernel, out_shape=(vmem((1024, 512), BF16), vmem((51...]
    unnamed x11 -> x0, local copies, waits for them, and re-layouts: 6.27 us -> none
    pallas_call x1 -> x0, local copies, waits for them, and re-layouts: 1.72 us -> none  [shards(): pl.pallas_call(fused_kernel, out_shape=(jax.ShapeDtypeStruct((1024, 512),...]
where the time goes in v3:
time: 51.7 us; the launch traced here: 51.6 us
  Pallas kernels  50.9 us (98%)
  between operations  0.64 us (1%)
    pallas_call x1, Pallas kernels, shards(): pl.pallas_call(fused_kernel, out_shape=(vmem((1024, 512), BF16), vmem((51...  49.4 us
    pallas_call x1, Pallas kernels, hand_over(): pl.pallas_call(copy_kernel, out_shape=tuple((jax.ShapeDtypeStruct(*shape)...  1.53 us

profile of v3, /device:TPU:1, one launch (start us, length us, event | category | flops | bytes accessed | tf_op | source)
XLA Modules:
  0.0 51.6 jit_solution(13412881157161363620)
XLA Ops:
  0.6 49.4 %fused.1 = (bf16[1024,512]{1,0:T(8,128)(2,1)S(1)}, bf16[512,512]{1,0:T(8,128)(2,1)S(1)}, f32[144,512]{1,0:T(8,128)S(1)}) custom-call(bf16[1024,512]{1,0:T(8,128)(2,1)} %embed_hbm.1, bf16[1024,512]{1,0:T(8,128)(2,1)} %cot_hbm.1, bf16[256,1024]{1,0:T(8,128)(2,1)} %bitcast.4, s32[16,1024]{1,0:T(8,128)} %index_hbm.1, s32[1,1024]{1,0:T(1,128)} %bitcast.6, ...), custom_call_target="tpu_custom_call" | custom-call | tf_op jit(solution)/shard_map/fused/pallas_call | solution.py:405
  50.0 1.5 %hand_over.1 = (bf16[1024,512]{1,0:T(8,128)(2,1)}, f32[512,512]{1,0:T(8,128)}, f32[64,512]{1,0:T(8,128)}, f32[64,512]{1,0:T(8,128)}, f32[16,64]{1,0:T(8,128)}) custom-call(bf16[1024,512]{1,0:T(8,128)(2,1)S(1)} %get-tuple-element.13.edge, bf16[512,512]{1,0:T(8,128)(2,1)S(1)} %get-tuple-element.14.res, f32[144,512]{1,0:T(8,128)S(1)} %get-tuple-element.15.small), custom_call_target="tpu_custom_call" | custom-call | tf_op jit(solution)/shard_map/hand_over/pallas_call | solution.py:390

commit v4 on v3

--- a/solution.py
+++ b/solution.py
@@ -83,13 +83,13 @@
         total = own[far]
         for s in range(15):
             total = total + got[s]
-        mid[near] = total
+        mid[near] = total.astype(mid.dtype)
 
     def final():
         spread.arrived()
-        total = mid[0]
+        total = mid[0].astype(F32)
         for s in range(1, 16):
-            total = total + mid[s]
+            total = total + mid[s].astype(F32)
         last[far] = total.astype(last.dtype)
 
     return scatter, middle, spread, final, gather
@@ -127,8 +127,8 @@
 
 def low_onehot(low):
     width = low.shape[1]
-    positions = lax.broadcasted_iota(jnp.int32, (256, width), 0)
-    return jnp.where(positions == low, 1.0, 0.0).astype(BF16)
+    positions = lax.broadcasted_iota(jnp.int32, (256, width), 0).astype(F32).astype(BF16)
+    return jnp.where(positions == low.astype(F32).astype(BF16), jnp.ones((), BF16), jnp.zeros((), BF16))
 
 
 def slice_of(s):
@@ -139,6 +139,7 @@
     embed_hbm, cot_hbm, basis_hbm, index_hbm, count_hbm, rows_hbm, w_res_hbm, down_hbm, w_up_hbm, w_basis_hbm,
     edge_hbm, res_hbm, small_out,
     embed, cot, basis, index, count, rows_out, w_res, down_t, w_up, w_basis,
+    w_block, terms, ghost_sum,
     table, pre, ghost_send, ghost_hot, dres, res_sum, wts, dsum,
     hot, picked, tsum, dt, table_sum, back_send, back_got, dpre,
     own_d, got_d, mid_d, last_d, own_u, got_u, mid_u, last_u, basis_got, basis_mid,
@@ -152,22 +153,27 @@
     behind = (ahead[1], ahead[0], ahead[3], ahead[2])
     loads = {}
     for place, (name, source, target) in enumerate((
-        ("embed", embed_hbm, embed), ("down", down_hbm, down_t), ("rows", rows_hbm, rows_out), ("w_res", w_res_hbm, w_res),
+        ("down", down_hbm, down_t), ("rows", rows_hbm, rows_out), ("w_res", w_res_hbm, w_res),
         ("cot", cot_hbm, cot), ("basis", basis_hbm, basis), ("w_basis", w_basis_hbm, w_basis), ("w_up", w_up_hbm, w_up),
         ("index", index_hbm, index), ("count", count_hbm, count),
     )):
         loads[name] = pltpu.make_async_copy(source, target, sem_in.at[place])
-    for name in ("embed", "down", "rows"):
-        loads[name].start()
+    quarters = [
+        pltpu.make_async_copy(embed_hbm.at[256 * c : 256 * c + 256, :], embed.at[256 * c : 256 * c + 256, :], sem_in.at[9 + c])
+        for c in range(4)
+    ]
+    loads["down"].start()
+    for quarter in quarters:
+        quarter.start()
+    loads["rows"].start()
     barrier = announce()
     for name in ("w_res", "cot", "basis", "w_basis", "w_up", "index", "count"):
         loads[name].start()
 
     loads["down"].wait()
-    loads["embed"].wait()
-    pre_all = dot(down_t[...], embed[...], 1, 1)
     for c in range(4):
-        part = pre_all[:, 256 * c : 256 * c + 256]
+        quarters[c].wait()
+        part = dot(down_t[...], embed[256 * c : 256 * c + 256, :], 1, 1)
         pre[64 * c : 64 * c + 64, :] = part
         table[64 * c : 64 * c + 64, :] = (part * sigmoid(part)).astype(BF16)
     loads["rows"].wait()
@@ -189,24 +195,24 @@
         value = dot(embed[rows, :], w_res[...])
         dres[rows, :] = (cot[rows, :].astype(F32) * silu_grad(value)).astype(BF16)
 
-    each(4, residual)
+    each(4, residual, 2)
+
+    pl.semaphore_wait(barrier, 32)
+
+    def ghost_copy(k):
+        place = table.at[pl.ds(256 + 64 * (k // 2), 64), pl.ds(128 * (k % 2), 128)]
+        return remote(ghost_send.at[k], place, sem_ghost.at[0], sem_ghost.at[1], ahead[k])
+
+    for k in range(4):
+        ghost_copy(k).start()
 
     def residual_grad(i):
         rows = pl.ds(pl.multiple_of(128 * i, 128), 128)
         res_sum[rows, :] = dot(embed[:, rows], dres[...], 0, 0)
 
-    each(4, residual_grad)
+    each(4, residual_grad, 2)
     other_half = pl.ds(pl.multiple_of((1 - core) * 256, 256), 256)
     half_send[...] = res_sum[other_half, :].astype(BF16)
-    pl.semaphore_wait(barrier, 32)
-
-    def ghost_copy(k):
-        place = table.at[pl.ds(256 + 64 * (k // 2), 64), pl.ds(128 * (k % 2), 128)]
-        return remote(ghost_send.at[k], place, sem_ghost.at[0], sem_ghost.at[1], ahead[k])
-
-    for k in range(4):
-        ghost_copy(k).start()
-
     core_first = remote(half_send, half_got, sem_core.at[0], sem_core.at[1], core_peer())
     core_first.start()
 
@@ -216,7 +222,13 @@
     wide_w = dot(w_basis[...], jnp.where(spread_n, 1.0, 0.0).astype(BF16), 0, 0)
     lane_slot = lax.broadcasted_iota(jnp.int32, (64, 256), 1) // 16
     for j in range(16):
-        wts[j] = dot(jnp.where(lane_slot == j, wide_w, 0.0).astype(BF16), basis[...])
+        w_block[64 * j : 64 * j + 64, :] = jnp.where(lane_slot == j, wide_w, 0.0).astype(BF16)
+
+    def slot_weights(i):
+        lanes = pl.ds(pl.multiple_of(256 * i, 256), 256)
+        wts[:, lanes] = dot(w_block[...], basis[:, lanes])
+
+    each(4, slot_weights, 2)
     dsum[...] = dot(w_up[...], cot[...], 1, 1)
 
     core_first.wait_recv()
@@ -233,7 +245,6 @@
     )
     res_scatter.start()
     pltpu.make_async_copy(ghost_send, ghost_send, sem_ghost.at[1]).wait()
-
     tsum[...] = jnp.zeros_like(tsum)
 
     def gather(j):
@@ -246,7 +257,7 @@
         for c in range(1, 6):
             chosen = jnp.where(chunk == c, wide[64 * c : 64 * c + 64], chosen)
         picked[j] = chosen.astype(BF16)
-        tsum[...] += wts[j] * chosen
+        tsum[...] += wts[pl.ds(pl.multiple_of(64 * j, 64), 64), :] * chosen
 
     each(16, gather, 2)
 
@@ -260,17 +271,31 @@
     scatter_u, middle_u, spread_u, final_u, gather_u = small_stages(own_u, got_u, mid_u, last_u, sems_u)
     scatter_u.start()
 
+    ghost_sum[...] = jnp.zeros_like(ghost_sum)
     table_sum[...] = jnp.zeros_like(table_sum)
 
-    def scatter(j):
+    def only(chunk, c):
+        return jnp.where(chunk == c, 1.0, 0.0).astype(BF16)
+
+    def scatter_ghosts(j):
         chunk = jnp.right_shift(index[pl.ds(j, 1), :], 8)
         slope = dt[...]
-        term = (slope * wts[j]).astype(BF16)
+        term = (slope * wts[pl.ds(pl.multiple_of(64 * j, 64), 64), :]).astype(BF16)
+        terms[j] = term
         picked[j] = (slope * picked[j].astype(F32)).astype(BF16)
-        parts = [term * jnp.where(chunk == c, 1.0, 0.0).astype(BF16) for c in range(6)]
-        table_sum[...] += dot(jnp.concatenate(parts, axis=0), hot[j], 1, 1)
-
-    each(8, scatter, 2)
+        parts = [term * only(chunk, c) for c in (4, 5)]
+        ghost_sum[...] += dot(hot[j], jnp.concatenate(parts, axis=0), 1, 1)
+
+    each(16, scatter_ghosts, 2)
+
+    def back_copy(k):
+        return remote(back_send.at[k], back_got.at[k], sem_back.at[0], sem_back.at[1], behind[k])
+
+    ghost_rows = ghost_sum[...].T
+    for k in range(4):
+        back_send[k] = ghost_rows[64 * (k // 2) : 64 * (k // 2) + 64, 128 * (k % 2) : 128 * (k % 2) + 128].astype(BF16)
+        back_copy(k).start()
+
     res_scatter.arrived()
     mine_far = pl.ds(pl.multiple_of(16 * far, 16), 16)
     part = res_sum[pl.ds(pl.multiple_of(mine + 16 * far, 16), 16), :] + half_got[mine_far, :].astype(F32)
@@ -279,36 +304,16 @@
     res_mid[z] = part.astype(BF16)
     res_spread = Exchange(7, lambda s: res_mid.at[z], lambda s: res_mid.at[z], res_mid.at[0:7], res_mid.at[0:7], (sem_z.at[0], sem_z.at[1]), z_peer)
     res_spread.start()
-    each(8, lambda j: scatter(j + 8), 2)
-
-    def back_copy(k):
-        return remote(back_send.at[k], back_got.at[k], sem_back.at[0], sem_back.at[1], behind[k])
-
-    for k in range(4):
-        back_send[k] = table_sum[256 + 64 * (k // 2) : 320 + 64 * (k // 2), 128 * (k % 2) : 128 * (k % 2) + 128].astype(BF16)
-        back_copy(k).start()
-
-    basis_grad = jnp.zeros((16, 64), F32)
-    for j in range(16):
-        basis_grad = basis_grad + dot(basis[16 * j : 16 * j + 16, :], picked[j], 1, 1)
-    basis_got[near] = basis_grad
-    basis_a = Exchange(15, lambda s: basis_got.at[near], lambda s: basis_got.at[near], basis_got.at[0:15], basis_got.at[0:15], (sem_basis.at[0, 0], sem_basis.at[1, 0]), near_peer)
-    basis_a.start()
-
     middle_u()
     spread_u.start()
-    res_spread.arrived()
-    part = res_mid[0].astype(F32)
-    for s in range(1, 8):
-        part = part + res_mid[s].astype(F32)
-    res_last[mine_far, :] = part.astype(BF16)
-    res_gather = Exchange(
-        15, lambda s: res_last.at[mine_far, :], lambda s: res_last.at[mine_far, :], res_last.at[0:240], res_last.at[0:240], (sem_far.at[0, 1], sem_far.at[1, 1]), far_peer
-    )
-    res_gather.start()
-
+    def scatter_own(j):
+        chunk = jnp.right_shift(index[pl.ds(j, 1), :], 8)
+        parts = [terms[j] * only(chunk, c) for c in range(4)]
+        table_sum[...] += dot(jnp.concatenate(parts, axis=0), hot[j], 1, 1)
+
+    each(16, scatter_own, 2)
     pltpu.make_async_copy(back_got, back_got, sem_back.at[1]).wait()
-    returned = table_sum[0:256, :]
+    returned = table_sum[...]
     for k in range(4):
         chunk = jnp.right_shift(rows_out[k : k + 1, :], 8)
         term = back_got[k]
@@ -324,15 +329,36 @@
     scatter_d, middle_d, spread_d, final_d, gather_d = small_stages(own_d, got_d, mid_d, last_d, sems_d)
     scatter_d.start()
 
+    basis_grad = jnp.zeros((16, 64), F32)
+    for j in range(16):
+        basis_grad = basis_grad + dot(basis[16 * j : 16 * j + 16, :], picked[j], 1, 1)
+    basis_got[near] = basis_grad
+    basis_a = Exchange(15, lambda s: basis_got.at[near], lambda s: basis_got.at[near], basis_got.at[0:15], basis_got.at[0:15], (sem_basis.at[0, 0], sem_basis.at[1, 0]), near_peer)
+    basis_a.start()
+
     def edge(i):
         rows = pl.ds(pl.multiple_of(256 * i, 256), 256)
         value = dot(dres[rows, :], w_res[...], 1, 1) + dot(dpre[:, rows], down_t[...], 0, 0)
         edge_out[rows, :] = value.astype(BF16)
 
-    each(4, edge)
+    each(4, edge, 2)
     edge_copy = pltpu.make_async_copy(edge_out, edge_hbm, sem_out.at[0])
     edge_copy.start()
 
+    middle_d()
+    spread_d.start()
+    res_spread.arrived()
+    part = res_mid[0].astype(F32)
+    for s in range(1, 8):
+        part = part + res_mid[s].astype(F32)
+    res_last[mine_far, :] = part.astype(BF16)
+    res_gather = Exchange(
+        15, lambda s: res_last.at[mine_far, :], lambda s: res_last.at[mine_far, :], res_last.at[0:240], res_last.at[0:240], (sem_far.at[0, 1], sem_far.at[1, 1]), far_peer
+    )
+    res_gather.start()
+
+    final_u()
+    gather_u.start()
     basis_a.arrived()
     basis_total = basis_got[0]
     for s in range(1, 16):
@@ -341,16 +367,12 @@
     basis_b = Exchange(15, lambda s: basis_mid.at[far], lambda s: basis_mid.at[far], basis_mid.at[0:15], basis_mid.at[0:15], (sem_basis.at[0, 1], sem_basis.at[1, 1]), far_peer)
     basis_b.start()
 
-    middle_d()
-    spread_d.start()
-    final_u()
-    gather_u.start()
+    final_d()
+    gather_d.start()
     res_gather.arrived()
     core_last = remote(res_last, res_other, sem_core.at[2], sem_core.at[3], core_peer())
     core_last.start()
     res_out[pl.ds(mine, 256), :] = res_last[...]
-    final_d()
-    gather_d.start()
     basis_b.arrived()
     basis_total = basis_mid[0]
     for s in range(1, 16):
@@ -422,29 +444,32 @@
             vmem((64, 512), BF16),
             vmem((64, 512), BF16),
             vmem((16, 64), BF16),
+            vmem((1024, 256), BF16),
+            vmem((16, 64, 1024), BF16),
+            vmem((256, 128), F32),
             vmem((384, 256), BF16),
             vmem((256, 256), F32),
             vmem((4, 64, 128), BF16),
             vmem((256, 512), BF16),
             vmem((1024, 512), BF16),
             vmem((512, 512), F32),
-            vmem((16, 64, 1024), F32),
+            vmem((1024, 1024), F32),
             vmem((64, 1024), F32),
             vmem((16, 256, 1024), BF16),
             vmem((16, 64, 1024), BF16),
             vmem((64, 1024), F32),
             vmem((64, 1024), F32),
-            vmem((384, 256), F32),
+            vmem((256, 256), F32),
             vmem((4, 64, 128), BF16),
             vmem((4, 64, 128), BF16),
             vmem((64, 1024), BF16),
             vmem((16, 8, 256), F32),
             vmem((15, 8, 256), F32),
-            vmem((16, 8, 256), F32),
+            vmem((16, 8, 256), BF16),
             vmem((16, 8, 256), BF16),
             vmem((16, 8, 256), F32),
             vmem((15, 8, 256), F32),
-            vmem((16, 8, 256), F32),
+            vmem((16, 8, 256), BF16),
             vmem((16, 8, 256), BF16),
             vmem((16, 16, 64), F32),
             vmem((16, 16, 64), F32),
@@ -463,7 +488,7 @@
             DMA((4,)),
             DMA((2,)),
             DMA((2, 2)),
-            DMA((10,)),
+            DMA((13,)),
             DMA((2,)),
             vmem((1024, 512), BF16),
             vmem((512, 512), BF16),

time: 51.7 us -> 47 us (0.909)
  Pallas kernels: 50.9 us -> 46.3 us
    pallas_call x1, Pallas kernels: 49.4 us -> 44.8 us  [shards(): pl.pallas_call(fused_kernel, out_shape=(vmem((1024, 512), BF16), vmem((51...]
where the time goes in v4:
time: 47 us; the launch traced here: 46.9 us
  Pallas kernels  46.3 us (99%)
  between operations  0.64 us (1%)
    pallas_call x1, Pallas kernels, shards(): pl.pallas_call(fused_kernel, out_shape=(vmem((1024, 512), BF16), vmem((51...  44.8 us
    pallas_call x1, Pallas kernels, hand_over(): pl.pallas_call(copy_kernel, out_shape=tuple((jax.ShapeDtypeStruct(*shape)...  1.53 us

profile of v4, /device:TPU:1, one launch (start us, length us, event | category | flops | bytes accessed | tf_op | source)
XLA Modules:
  0.0 46.9 jit_solution(18261110463077920694)
XLA Ops:
  0.6 44.8 %fused.1 = (bf16[1024,512]{1,0:T(8,128)(2,1)S(1)}, bf16[512,512]{1,0:T(8,128)(2,1)S(1)}, f32[144,512]{1,0:T(8,128)S(1)}) custom-call(bf16[1024,512]{1,0:T(8,128)(2,1)} %embed_hbm.1, bf16[1024,512]{1,0:T(8,128)(2,1)} %cot_hbm.1, bf16[256,1024]{1,0:T(8,128)(2,1)} %bitcast.4, s32[16,1024]{1,0:T(8,128)} %index_hbm.1, s32[1,1024]{1,0:T(1,128)} %bitcast.6, ...), custom_call_target="tpu_custom_call" | custom-call | tf_op jit(solution)/shard_map/fused/pallas_call | solution.py:427
  45.4 1.5 %hand_over.1 = (bf16[1024,512]{1,0:T(8,128)(2,1)}, f32[512,512]{1,0:T(8,128)}, f32[64,512]{1,0:T(8,128)}, f32[64,512]{1,0:T(8,128)}, f32[16,64]{1,0:T(8,128)}) custom-call(bf16[1024,512]{1,0:T(8,128)(2,1)S(1)} %get-tuple-element.13.edge, bf16[512,512]{1,0:T(8,128)(2,1)S(1)} %get-tuple-element.14.res, f32[144,512]{1,0:T(8,128)S(1)} %get-tuple-element.15.small), custom_call_target="tpu_custom_call" | custom-call | tf_op jit(solution)/shard_map/hand_over/pallas_call | solution.py:412

commit v5 on v4

--- a/solution.py
+++ b/solution.py
@@ -137,14 +137,14 @@
 
 def fused_kernel(
     embed_hbm, cot_hbm, basis_hbm, index_hbm, count_hbm, rows_hbm, w_res_hbm, down_hbm, w_up_hbm, w_basis_hbm,
-    edge_hbm, res_hbm, small_out,
+    edge_hbm, res_hbm, small_out, basis_dest,
     embed, cot, basis, index, count, rows_out, w_res, down_t, w_up, w_basis,
-    w_block, terms, ghost_sum,
+    terms, ghost_sum,
     table, pre, ghost_send, ghost_hot, dres, res_sum, wts, dsum,
     hot, picked, tsum, dt, table_sum, back_send, back_got, dpre,
     own_d, got_d, mid_d, last_d, own_u, got_u, mid_u, last_u, basis_got, basis_mid,
     half_send, half_got, far_send, far_got, res_mid, res_last, res_other,
-    sem_ghost, sem_back, sem_d, sem_u, sem_basis, sem_core, sem_z, sem_far, sem_in, sem_out, edge_out, res_out,
+    sem_ghost, sem_back, sem_d, sem_u, sem_basis, sem_core, sem_z, sem_far, sem_in, sem_out, edge_out, res_out, basis_out,
 ):
     slab, brick, near, far = where_am_i()
     core, z = lax.rem(near, 2), near // 2
@@ -165,8 +165,8 @@
     loads["down"].start()
     for quarter in quarters:
         quarter.start()
+    barrier = announce()
     loads["rows"].start()
-    barrier = announce()
     for name in ("w_res", "cot", "basis", "w_basis", "w_up", "index", "count"):
         loads[name].start()
 
@@ -187,6 +187,15 @@
         for c in range(1, 4):
             chosen = jnp.where(chunk == c, wide[64 * c : 64 * c + 64], chosen)
         ghost_send[k] = chosen.astype(BF16)
+    pl.semaphore_wait(barrier, 32)
+
+    def ghost_copy(k):
+        place = table.at[pl.ds(256 + 64 * (k // 2), 64), pl.ds(128 * (k % 2), 128)]
+        return remote(ghost_send.at[k], place, sem_ghost.at[0], sem_ghost.at[1], ahead[k])
+
+    for k in range(4):
+        ghost_copy(k).start()
+
     loads["w_res"].wait()
     loads["cot"].wait()
 
@@ -196,15 +205,6 @@
         dres[rows, :] = (cot[rows, :].astype(F32) * silu_grad(value)).astype(BF16)
 
     each(4, residual, 2)
-
-    pl.semaphore_wait(barrier, 32)
-
-    def ghost_copy(k):
-        place = table.at[pl.ds(256 + 64 * (k // 2), 64), pl.ds(128 * (k % 2), 128)]
-        return remote(ghost_send.at[k], place, sem_ghost.at[0], sem_ghost.at[1], ahead[k])
-
-    for k in range(4):
-        ghost_copy(k).start()
 
     def residual_grad(i):
         rows = pl.ds(pl.multiple_of(128 * i, 128), 128)
@@ -218,32 +218,9 @@
 
     for name in ("basis", "w_basis", "w_up", "index", "count"):
         loads[name].wait()
-    spread_n = (lax.broadcasted_iota(jnp.int32, (16, 256), 1) % 16) == lax.broadcasted_iota(jnp.int32, (16, 256), 0)
-    wide_w = dot(w_basis[...], jnp.where(spread_n, 1.0, 0.0).astype(BF16), 0, 0)
-    lane_slot = lax.broadcasted_iota(jnp.int32, (64, 256), 1) // 16
-    for j in range(16):
-        w_block[64 * j : 64 * j + 64, :] = jnp.where(lane_slot == j, wide_w, 0.0).astype(BF16)
-
-    def slot_weights(i):
-        lanes = pl.ds(pl.multiple_of(256 * i, 256), 256)
-        wts[:, lanes] = dot(w_block[...], basis[:, lanes])
-
-    each(4, slot_weights, 2)
+    w_t = w_basis[...].T
     dsum[...] = dot(w_up[...], cot[...], 1, 1)
 
-    core_first.wait_recv()
-    mine = pl.multiple_of(core * 256, 256)
-
-    def to_far(t):
-        rows = pl.ds(pl.multiple_of(mine + 16 * t, 16), 16)
-        got = half_got[pl.ds(pl.multiple_of(16 * t, 16), 16), :]
-        far_send[t] = (res_sum[rows, :] + got.astype(F32)).astype(BF16)
-
-    each(16, to_far)
-    res_scatter = Exchange(
-        15, lambda s: far_send.at[lax.rem(far + s + 1, 16)], lambda s: far_got.at[s], far_got, far_got, (sem_far.at[0, 0], sem_far.at[1, 0]), far_peer
-    )
-    res_scatter.start()
     pltpu.make_async_copy(ghost_send, ghost_send, sem_ghost.at[1]).wait()
     tsum[...] = jnp.zeros_like(tsum)
 
@@ -257,20 +234,29 @@
         for c in range(1, 6):
             chosen = jnp.where(chunk == c, wide[64 * c : 64 * c + 64], chosen)
         picked[j] = chosen.astype(BF16)
-        tsum[...] += wts[pl.ds(pl.multiple_of(64 * j, 64), 64), :] * chosen
-
-    each(16, gather, 2)
+        weights = dot(w_t, basis[pl.ds(pl.multiple_of(16 * j, 16), 16), :])
+        wts[pl.ds(pl.multiple_of(64 * j, 64), 64), :] = weights
+        tsum[...] += weights * chosen
+
+    each(4, gather, 4)
+    core_first.wait_recv()
+    mine = pl.multiple_of(core * 256, 256)
+
+    def to_far(t):
+        rows = pl.ds(pl.multiple_of(mine + 16 * t, 16), 16)
+        got = half_got[pl.ds(pl.multiple_of(16 * t, 16), 16), :]
+        far_send[t] = (res_sum[rows, :] + got.astype(F32)).astype(BF16)
+
+    each(16, to_far)
+    res_scatter = Exchange(
+        15, lambda s: far_send.at[lax.rem(far + s + 1, 16)], lambda s: far_got.at[s], far_got, far_got, (sem_far.at[0, 0], sem_far.at[1, 0]), far_peer
+    )
+    res_scatter.start()
+    each(12, lambda j: gather(j + 4), 4)
 
     total = tsum[...]
     act = (total * sigmoid(total)).astype(BF16)
     dt[...] = dsum[...] * silu_grad(total)
-    up_grad = dot(act, cot[...])
-    for s in range(16):
-        own_u[s] = up_grad[8 * (s // 2) : 8 * (s // 2) + 8, 256 * (s % 2) : 256 * (s % 2) + 256]
-    sems_u = [(sem_u.at[0, t], sem_u.at[1, t]) for t in range(3)]
-    scatter_u, middle_u, spread_u, final_u, gather_u = small_stages(own_u, got_u, mid_u, last_u, sems_u)
-    scatter_u.start()
-
     ghost_sum[...] = jnp.zeros_like(ghost_sum)
     table_sum[...] = jnp.zeros_like(table_sum)
 
@@ -286,7 +272,7 @@
         parts = [term * only(chunk, c) for c in (4, 5)]
         ghost_sum[...] += dot(hot[j], jnp.concatenate(parts, axis=0), 1, 1)
 
-    each(16, scatter_ghosts, 2)
+    each(16, scatter_ghosts, 8)
 
     def back_copy(k):
         return remote(back_send.at[k], back_got.at[k], sem_back.at[0], sem_back.at[1], behind[k])
@@ -295,6 +281,13 @@
     for k in range(4):
         back_send[k] = ghost_rows[64 * (k // 2) : 64 * (k // 2) + 64, 128 * (k % 2) : 128 * (k % 2) + 128].astype(BF16)
         back_copy(k).start()
+
+    up_grad = dot(act, cot[...])
+    for s in range(16):
+        own_u[s] = up_grad[8 * (s // 2) : 8 * (s // 2) + 8, 256 * (s % 2) : 256 * (s % 2) + 256]
+    sems_u = [(sem_u.at[0, t], sem_u.at[1, t]) for t in range(3)]
+    scatter_u, middle_u, spread_u, final_u, gather_u = small_stages(own_u, got_u, mid_u, last_u, sems_u)
+    scatter_u.start()
 
     res_scatter.arrived()
     mine_far = pl.ds(pl.multiple_of(16 * far, 16), 16)
@@ -304,21 +297,26 @@
     res_mid[z] = part.astype(BF16)
     res_spread = Exchange(7, lambda s: res_mid.at[z], lambda s: res_mid.at[z], res_mid.at[0:7], res_mid.at[0:7], (sem_z.at[0], sem_z.at[1]), z_peer)
     res_spread.start()
-    middle_u()
-    spread_u.start()
     def scatter_own(j):
         chunk = jnp.right_shift(index[pl.ds(j, 1), :], 8)
         parts = [terms[j] * only(chunk, c) for c in range(4)]
         table_sum[...] += dot(jnp.concatenate(parts, axis=0), hot[j], 1, 1)
 
-    each(16, scatter_own, 2)
+    each(16, scatter_own, 8)
+    basis_grad = jnp.zeros((16, 64), F32)
+    for j in range(16):
+        basis_grad = basis_grad + dot(basis[16 * j : 16 * j + 16, :], picked[j], 1, 1)
+    basis_got[near] = jnp.concatenate([basis_grad[0:8], basis_grad[8:16]], axis=1)
+    basis_a = Exchange(15, lambda s: basis_got.at[near], lambda s: basis_got.at[near], basis_got.at[0:15], basis_got.at[0:15], (sem_basis.at[0, 0], sem_basis.at[1, 0]), near_peer)
+    basis_a.start()
+
     pltpu.make_async_copy(back_got, back_got, sem_back.at[1]).wait()
-    returned = table_sum[...]
+    columns = []
     for k in range(4):
         chunk = jnp.right_shift(rows_out[k : k + 1, :], 8)
         term = back_got[k]
-        parts = [term * jnp.where(chunk == c, 1.0, 0.0).astype(BF16) for c in range(4)]
-        returned = returned + dot(jnp.concatenate(parts, axis=0), ghost_hot[:, 128 * k : 128 * k + 128], 1, 1)
+        columns.append(jnp.concatenate([term * only(chunk, c) for c in range(4)], axis=0))
+    returned = table_sum[...] + dot(jnp.concatenate(columns, axis=1), ghost_hot[...], 1, 1)
     returned = (returned * silu_grad(pre[...])).astype(BF16)
     for c in range(4):
         dpre[:, 256 * c : 256 * c + 256] = returned[64 * c : 64 * c + 64, :]
@@ -329,13 +327,6 @@
     scatter_d, middle_d, spread_d, final_d, gather_d = small_stages(own_d, got_d, mid_d, last_d, sems_d)
     scatter_d.start()
 
-    basis_grad = jnp.zeros((16, 64), F32)
-    for j in range(16):
-        basis_grad = basis_grad + dot(basis[16 * j : 16 * j + 16, :], picked[j], 1, 1)
-    basis_got[near] = basis_grad
-    basis_a = Exchange(15, lambda s: basis_got.at[near], lambda s: basis_got.at[near], basis_got.at[0:15], basis_got.at[0:15], (sem_basis.at[0, 0], sem_basis.at[1, 0]), near_peer)
-    basis_a.start()
-
     def edge(i):
         rows = pl.ds(pl.multiple_of(256 * i, 256), 256)
         value = dot(dres[rows, :], w_res[...], 1, 1) + dot(dpre[:, rows], down_t[...], 0, 0)
@@ -345,6 +336,8 @@
     edge_copy = pltpu.make_async_copy(edge_out, edge_hbm, sem_out.at[0])
     edge_copy.start()
 
+    middle_u()
+    spread_u.start()
     middle_d()
     spread_d.start()
     res_spread.arrived()
@@ -372,17 +365,19 @@
     res_gather.arrived()
     core_last = remote(res_last, res_other, sem_core.at[2], sem_core.at[3], core_peer())
     core_last.start()
-    res_out[pl.ds(mine, 256), :] = res_last[...]
+    res_out[pl.ds(mine, 256), :] = res_last[...].astype(F32)
     basis_b.arrived()
     basis_total = basis_mid[0]
     for s in range(1, 16):
         basis_total = basis_total + basis_mid[s]
-    small_out[128:144, 0:64] = basis_total
+    basis_out[...] = jnp.concatenate([basis_total[:, 0:64], basis_total[:, 64:128]], axis=0)
+    basis_copy = pltpu.make_async_copy(basis_out, basis_dest, sem_out.at[2])
+    basis_copy.start()
     gather_u.arrived()
     for s in range(16):
         small_out[64 + 8 * (s // 2) : 72 + 8 * (s // 2), 256 * (s % 2) : 256 * (s % 2) + 256] = last_u[s].astype(F32)
     core_last.wait_recv()
-    res_out[other_half, :] = res_other[...]
+    res_out[other_half, :] = res_other[...].astype(F32)
     res_copy = pltpu.make_async_copy(res_out, res_hbm, sem_out.at[1])
     res_copy.start()
     pltpu.make_async_copy(ghost_send, ghost_send, sem_ghost.at[0]).wait()
@@ -397,26 +392,32 @@
     gather_d.sent()
     edge_copy.wait()
     res_copy.wait()
-
-
-def copy_kernel(edge, res, small, edge_out, res_out, down_out, up_out, basis_out):
-    edge_out[...] = edge[...]
-    res_out[...] = res[...].astype(F32)
-    down_out[...] = small[0:64, :]
-    up_out[...] = small[64:128, :]
-    basis_out[...] = small[128:144, 0:64]
-
-
-def hand_over(edge, res, small):
+    basis_copy.wait()
+
+
+def copy_kernel(edge, res, small, basis, edge_out, res_out, down_out, up_out, basis_out, sems):
+    pairs = [(small.at[0:64, :], down_out), (small.at[64:128, :], up_out), (basis, basis_out)]
+    for k in range(4):
+        pairs.append((edge.at[256 * k : 256 * k + 256, :], edge_out.at[256 * k : 256 * k + 256, :]))
+        pairs.append((res.at[128 * k : 128 * k + 128, :], res_out.at[128 * k : 128 * k + 128, :]))
+    copies = [pltpu.make_async_copy(source, target, sems.at[k]) for k, (source, target) in enumerate(pairs)]
+    for copy in copies:
+        copy.start()
+    for copy in copies:
+        copy.wait()
+
+
+def hand_over(edge, res, small, basis):
     shapes = (((1024, 512), BF16), ((512, 512), F32), ((64, 512), F32), ((64, 512), F32), ((16, 64), F32))
     return pl.pallas_call(
         copy_kernel,
         out_shape=tuple(jax.ShapeDtypeStruct(*shape) for shape in shapes),
-        in_specs=[pl.BlockSpec(memory_space=pltpu.VMEM)] * 3,
-        out_specs=[pl.BlockSpec(memory_space=pltpu.VMEM)] * 5,
+        in_specs=[pl.BlockSpec(memory_space=pl.ANY)] * 4,
+        out_specs=[pl.BlockSpec(memory_space=pl.ANY)] * 5,
+        scratch_shapes=[DMA((11,))],
         compiler_params=pltpu.CompilerParams(vmem_limit_bytes=8 * 1024 * 1024),
         name="hand_over",
-    )(edge, res, small)
+    )(edge, res, small, basis)
 
 
 def shards(
@@ -424,15 +425,16 @@
     residual_weight, down_weight, up_weight, basis_weight,
 ):
     vmem = pltpu.VMEM
-    edge, res, small = pl.pallas_call(
+    edge, res, small, base = pl.pallas_call(
         fused_kernel,
         out_shape=(
             vmem((1024, 512), BF16),
-            vmem((512, 512), BF16),
-            vmem((144, 512), F32),
+            vmem((512, 512), F32),
+            vmem((128, 512), F32),
+            vmem((16, 64), F32),
         ),
         in_specs=[pl.BlockSpec(memory_space=pltpu.HBM)] * 10,
-        out_specs=[pl.BlockSpec(memory_space=pl.ANY), pl.BlockSpec(memory_space=pl.ANY), pl.BlockSpec(memory_space=vmem)],
+        out_specs=[pl.BlockSpec(memory_space=pl.ANY), pl.BlockSpec(memory_space=pl.ANY), pl.BlockSpec(memory_space=vmem), pl.BlockSpec(memory_space=pl.ANY)],
         scratch_shapes=[
             vmem((1024, 512), BF16),
             vmem((1024, 512), BF16),
@@ -444,7 +446,6 @@
             vmem((64, 512), BF16),
             vmem((64, 512), BF16),
             vmem((16, 64), BF16),
-            vmem((1024, 256), BF16),
             vmem((16, 64, 1024), BF16),
             vmem((256, 128), F32),
             vmem((384, 256), BF16),
@@ -471,8 +472,8 @@
             vmem((15, 8, 256), F32),
             vmem((16, 8, 256), BF16),
             vmem((16, 8, 256), BF16),
-            vmem((16, 16, 64), F32),
-            vmem((16, 16, 64), F32),
+            vmem((16, 8, 128), F32),
+            vmem((16, 8, 128), F32),
             vmem((256, 512), BF16),
             vmem((256, 512), BF16),
             vmem((16, 16, 512), BF16),
@@ -489,9 +490,10 @@
             DMA((2,)),
             DMA((2, 2)),
             DMA((13,)),
-            DMA((2,)),
+            DMA((3,)),
             vmem((1024, 512), BF16),
-            vmem((512, 512), BF16),
+            vmem((512, 512), F32),
+            vmem((16, 64), F32),
         ],
         compiler_params=pltpu.CompilerParams(
             collective_id=0, has_side_effects=True, vmem_limit_bytes=40 * 1024 * 1024
@@ -506,7 +508,7 @@
             )
         )
     )
-    edge, res, down, up, base = hand_over(edge, res, small)
+    edge, res, down, up, base = hand_over(edge, res, small, base)
     return edge, res, down.T, up, base
 
 

time: 47 us -> 45.3 us (0.964)
  Pallas kernels: 46.3 us -> 44.6 us
    pallas_call x1, Pallas kernels: 44.8 us -> 43.1 us  [shards(): pl.pallas_call(fused_kernel, out_shape=(vmem((1024, 512), BF16), vmem((51...]
where the time goes in v5:
time: 45.3 us; the launch traced here: 45.2 us
  Pallas kernels  44.6 us (98%)
  between operations  0.64 us (1%)
    pallas_call x1, Pallas kernels, shards(): pl.pallas_call(fused_kernel, out_shape=(vmem((1024, 512), BF16), vmem((51...  43.1 us
    pallas_call x1, Pallas kernels, hand_over(): pl.pallas_call(copy_kernel, out_shape=tuple((jax.ShapeDtypeStruct(*shape)...  1.49 us

profile of v5, /device:TPU:1, one launch (start us, length us, event | category | flops | bytes accessed | tf_op | source)
XLA Modules:
  0.0 45.2 jit_solution(2526685515521128169)
XLA Ops:
  0.6 43.1 %fused.1 = (bf16[1024,512]{1,0:T(8,128)(2,1)S(1)}, f32[512,512]{1,0:T(8,128)S(1)}, f32[128,512]{1,0:T(8,128)S(1)}, f32[16,64]{1,0:T(8,128)S(1)}) custom-call(bf16[1024,512]{1,0:T(8,128)(2,1)} %embed_hbm.1, bf16[1024,512]{1,0:T(8,128)(2,1)} %cot_hbm.1, bf16[256,1024]{1,0:T(8,128)(2,1)} %bitcast.4, s32[16,1024]{1,0:T(8,128)} %index_hbm.1, s32[1,1024]{1,0:T(1,128)} %bitcast.6, ...), custom_call_target="tpu_custom_call" | custom-call | tf_op jit(solution)/shard_map/fused/pallas_call | solution.py:428
  43.7 1.5 %hand_over.1 = (bf16[1024,512]{1,0:T(8,128)(2,1)}, f32[512,512]{1,0:T(8,128)}, f32[64,512]{1,0:T(8,128)}, f32[64,512]{1,0:T(8,128)}, f32[16,64]{1,0:T(8,128)}) custom-call(bf16[1024,512]{1,0:T(8,128)(2,1)S(1)} %get-tuple-element.14.edge, f32[512,512]{1,0:T(8,128)S(1)} %get-tuple-element.15.res, f32[128,512]{1,0:T(8,128)S(1)} %get-tuple-element.16.small, ...), custom_call_target="tpu_custom_call" | custom-call | tf_op jit(solution)/shard_map/hand_over/pallas_call | solution.py:412

commit v6 on v5

--- a/solution.py
+++ b/solution.py
@@ -54,6 +54,13 @@
     lax.fori_loop(0, count, step, 0, unroll=unroll)
 
 
+FARTHEST_FIRST = {
+    near_peer: (8, 7, 9, 6, 10, 5, 11, 4, 12, 3, 13, 2, 14, 1, 15),
+    far_peer: (3, 13, 5, 11, 4, 12, 1, 15, 6, 10, 7, 9, 2, 14, 8),
+    z_peer: (4, 3, 5, 2, 6, 1, 7),
+}
+
+
 class Exchange:
     def __init__(self, count, source, target, gone, came, sems, peer):
         self.count, self.source, self.target, self.gone, self.came = count, source, target, gone, came
@@ -61,7 +68,9 @@
 
     def start(self):
         send, recv = self.sems
-        each(self.count, lambda s: remote(self.source(s), self.target(s), send, recv, self.peer(s + 1)).start())
+        for step in FARTHEST_FIRST[self.peer]:
+            s = step - 1
+            remote(self.source(s), self.target(s), send, recv, self.peer(step)).start()
 
     def arrived(self):
         pltpu.make_async_copy(self.came, self.came, self.sems[1]).wait()
@@ -102,8 +111,9 @@
     def tell(peer):
         pl.semaphore_signal(barrier, inc=1, device_id=peer, device_id_type=MESH)
 
-    each(15, lambda s: tell(near_peer(s + 1)))
-    each(15, lambda s: tell(far_peer(s + 1)))
+    for peer in (near_peer, far_peer):
+        for step in FARTHEST_FIRST[peer]:
+            tell(peer(step))
     tell((slab, lax.rem(brick + 1, 32)))
     tell((slab, lax.rem(brick + 31, 32)))
     return barrier
@@ -193,7 +203,7 @@
         place = table.at[pl.ds(256 + 64 * (k // 2), 64), pl.ds(128 * (k % 2), 128)]
         return remote(ghost_send.at[k], place, sem_ghost.at[0], sem_ghost.at[1], ahead[k])
 
-    for k in range(4):
+    for k in (2, 3, 0, 1):
         ghost_copy(k).start()
 
     loads["w_res"].wait()
@@ -278,7 +288,7 @@
         return remote(back_send.at[k], back_got.at[k], sem_back.at[0], sem_back.at[1], behind[k])
 
     ghost_rows = ghost_sum[...].T
-    for k in range(4):
+    for k in (2, 3, 0, 1):
         back_send[k] = ghost_rows[64 * (k // 2) : 64 * (k // 2) + 64, 128 * (k % 2) : 128 * (k % 2) + 128].astype(BF16)
         back_copy(k).start()
 

time: 45.3 us -> 44.1 us (0.974)
  Pallas kernels: 44.6 us -> 43.4 us
    pallas_call x1, Pallas kernels: 43.1 us -> 41.9 us  [shards(): pl.pallas_call(fused_kernel, out_shape=(vmem((1024, 512), BF16), vmem((51...]
where the time goes in v6:
time: 44.1 us; the launch traced here: 44 us
  Pallas kernels  43.4 us (98%)
  between operations  0.64 us (1%)
    pallas_call x1, Pallas kernels, shards(): pl.pallas_call(fused_kernel, out_shape=(vmem((1024, 512), BF16), vmem((51...  41.9 us
    pallas_call x1, Pallas kernels, hand_over(): pl.pallas_call(copy_kernel, out_shape=tuple((jax.ShapeDtypeStruct(*shape)...  1.49 us

profile of v6, /device:TPU:1, one launch (start us, length us, event | category | flops | bytes accessed | tf_op | source)
XLA Modules:
  0.0 44.0 jit_solution(9840221442068427558)
XLA Ops:
  0.6 41.9 %fused.1 = (bf16[1024,512]{1,0:T(8,128)(2,1)S(1)}, f32[512,512]{1,0:T(8,128)S(1)}, f32[128,512]{1,0:T(8,128)S(1)}, f32[16,64]{1,0:T(8,128)S(1)}) custom-call(bf16[1024,512]{1,0:T(8,128)(2,1)} %embed_hbm.1, bf16[1024,512]{1,0:T(8,128)(2,1)} %cot_hbm.1, bf16[256,1024]{1,0:T(8,128)(2,1)} %bitcast.4, s32[16,1024]{1,0:T(8,128)} %index_hbm.1, s32[1,1024]{1,0:T(1,128)} %bitcast.6, ...), custom_call_target="tpu_custom_call" | custom-call | tf_op jit(solution)/shard_map/fused/pallas_call | solution.py:438
  42.5 1.5 %hand_over.1 = (bf16[1024,512]{1,0:T(8,128)(2,1)}, f32[512,512]{1,0:T(8,128)}, f32[64,512]{1,0:T(8,128)}, f32[64,512]{1,0:T(8,128)}, f32[16,64]{1,0:T(8,128)}) custom-call(bf16[1024,512]{1,0:T(8,128)(2,1)S(1)} %get-tuple-element.14.edge, f32[512,512]{1,0:T(8,128)S(1)} %get-tuple-element.15.res, f32[128,512]{1,0:T(8,128)S(1)} %get-tuple-element.16.small, ...), custom_call_target="tpu_custom_call" | custom-call | tf_op jit(solution)/shard_map/hand_over/pallas_call | solution.py:422
